TPU v7x, 32 devices: a whole 2x2x4 slice. The times are simulated.
32 devices in a mesh: group: 2 (over x), seq: 16 (over z, y, core).
Axes of the slice: x: 2, y: 2, z: 4, core: 2. Of those that a mesh axis runs over, the one named last changes fastest.
Arguments:
- queries: bfloat16 [96, 128, 2560], P(('group', 'seq')), parts along dimension 0, may hold values from -9 to 9
- keys: bfloat16 [96, 128, 2560], P(('group', 'seq')), parts along dimension 0, may hold values from -9 to 9
- values: bfloat16 [96, 128, 2560], P(('group', 'seq')), parts along dimension 0, may hold values from -6 to 6
- block_list: int32 [96, 20, 2], P('group'), parts along dimension 0, may hold values from 0 to 47, as said below
- list_len: int32 [96, 20], P('group'), parts along dimension 0, may hold values from 0 to 2, as said below
- window_time: int32 [20], replicated, may hold values from 0 to 1
- window_rows: int32 [20], replicated, may hold values from 0 to 1
Outputs:
- attention_out: bfloat16 [96, 128, 2560], P(('group', 'seq')), parts along dimension 0
There are 2 independent parts, one for each index of `group`. A program takes and returns all parts, laid end to end along the dimension named above; an argument that names none is the same for every part. Nothing has to cross between parts.
Inputs may be any that keep to these rules, and one draw needn't show every extreme that they name: `block_list`: for the 3 query tiles of one block and one head, all listed tiles lie on a single other block, and together the used entries name exactly 2 distinct tiles; one list's entries are distinct. For the query tiles of one block, no other block holds listed tiles of more than 2 heads, and some block holds those of exactly 2 heads, so the distinct listed pairs of tile and head of one block on another block number at most 4, reached in every draw. Entries of block_list at and after position list_len are not used.
All inputs are finite; a program needn't handle non-finite values.
Results may differ from a plain program's by a relative error of at most 0.0032.
Values may be sent and summed in bfloat16 or wider, within the bound.
No kernel may reach another device: no remote copies, remote signals or barrier semaphores. Data moves between devices by JAX's collectives and lax.ppermute only.
A program may use at most 128 MiB of HBM per device.

v0:
```python
import math

import jax
import jax.numpy as jnp
from jax import lax
from jax.sharding import PartitionSpec as P

TIME_TILES = 1
ROW_TILES = 3
ROW_BLOCKS = 2
LIST = 2


BIG_NEG = -1e30


def from_partner(block, axis, apart):
    count = lax.axis_size(axis)
    route = []
    for low in range(count):
        high = low | 1 << apart
        if high != low and high < count:
            route += [(low, high), (high, low)]
    return lax.ppermute(block, axis, route)


def passed_along(value, axis, steps):
    count = lax.axis_size(axis)
    initial, last = (max(0, -steps), min(count, count - steps))
    return lax.ppermute(value, axis, [(source, source + steps) for source in range(initial, last)])


def halo_paired(key_block, val_block, row_pos):
    edge_key = jnp.where(row_pos == 0, key_block[:, ROW_TILES - 1], key_block[:, 0])
    edge_val = jnp.where(row_pos == 0, val_block[:, ROW_TILES - 1], val_block[:, 0])
    got_key, got_val = from_partner((edge_key, edge_val), "seq", 0)
    middle_shape = (TIME_TILES, ROW_TILES + 2) + key_block.shape[2:]
    middle_key = jnp.zeros(middle_shape, key_block.dtype).at[:, 1 : ROW_TILES + 1].set(key_block)
    middle_val = jnp.zeros(middle_shape, val_block.dtype).at[:, 1 : ROW_TILES + 1].set(val_block)
    blank_key = jnp.zeros_like(got_key)
    blank_val = jnp.zeros_like(got_val)
    middle_key = middle_key.at[:, 0].set(jnp.where(row_pos == 1, got_key, blank_key))
    middle_val = middle_val.at[:, 0].set(jnp.where(row_pos == 1, got_val, blank_val))
    middle_key = middle_key.at[:, ROW_TILES + 1].set(jnp.where(row_pos == 0, got_key, blank_key))
    middle_val = middle_val.at[:, ROW_TILES + 1].set(jnp.where(row_pos == 0, got_val, blank_val))
    start = jnp.where(row_pos == 0, 1, 0).astype(jnp.int32)
    shape = (TIME_TILES + 2, ROW_TILES + 2) + key_block.shape[2:]
    key_ext = jnp.zeros(shape, key_block.dtype).at[1 : TIME_TILES + 1].set(middle_key)
    val_ext = jnp.zeros(shape, val_block.dtype).at[1 : TIME_TILES + 1].set(middle_val)
    zero_index = jnp.int32(0)
    for distance, source, target in (
        (ROW_BLOCKS, TIME_TILES - 1, 0),
        (-ROW_BLOCKS, 0, TIME_TILES + 1),
    ):
        band_key = lax.dynamic_slice_in_dim(middle_key, start, ROW_TILES + 1, 1)
        band_val = lax.dynamic_slice_in_dim(middle_val, start, ROW_TILES + 1, 1)
        recv_key, recv_val = passed_along((band_key, band_val), "seq", distance)
        where_to = (jnp.int32(target), start, zero_index, zero_index)
        key_ext = lax.dynamic_update_slice(key_ext, recv_key, where_to)
        val_ext = lax.dynamic_update_slice(val_ext, recv_val, where_to)
    return (key_ext, val_ext)


def on_device(queries, keys, values, block_list, list_len, window_time, window_rows):
    tiles_dev, tile_len, feat = queries.shape
    heads = window_time.shape[0]
    head_dim = feat // heads
    tiles_total = block_list.shape[0]
    blocks = lax.axis_size("seq")
    device = lax.axis_index("seq")
    time_block = device // ROW_BLOCKS
    row_pos = device % ROW_BLOCKS
    key_block = keys.reshape((TIME_TILES, ROW_TILES) + keys.shape[1:])
    val_block = values.reshape((TIME_TILES, ROW_TILES) + values.shape[1:])
    key_ext, val_ext = halo_paired(key_block, val_block, row_pos)
    time_count = TIME_TILES * blocks // ROW_BLOCKS
    row_count = ROW_BLOCKS * ROW_TILES
    ext_cols = ROW_TILES + 2
    ext_time = time_block * TIME_TILES + jnp.arange(TIME_TILES + 2, dtype=jnp.int32) - 1
    ext_row = row_pos * ROW_TILES + jnp.arange(ext_cols, dtype=jnp.int32) - 1
    ext_valid = ((ext_time >= 0) & (ext_time < time_count))[:, None] & (
        (ext_row >= 0) & (ext_row < row_count)
    )[None, :]
    valid_rows = jnp.stack([ext_valid[a : a + TIME_TILES] for a in range(3)], axis=1)
    col_gap = jnp.abs(
        jnp.arange(ext_cols, dtype=jnp.int32)[None, :]
        - jnp.arange(ROW_TILES, dtype=jnp.int32)[:, None]
        - 1
    )
    time_gap = jnp.abs(jnp.arange(3, dtype=jnp.int32) - 1)
    far_min = blocks - 1
    per_source = (heads + far_min - 1) // far_min
    capacity = per_source * LIST
    pair_count = heads * tiles_dev
    all_live = jnp.arange(LIST, dtype=jnp.int32)[None, None, :] < list_len[:, :, None]
    local_ids = block_list - device * tiles_dev
    mine = all_live & (local_ids >= 0) & (local_ids < tiles_dev)
    wanted = (local_ids[..., None] == jnp.arange(tiles_dev, dtype=jnp.int32)) & mine[..., None]
    wanted = jnp.any(wanted, axis=2).reshape(blocks, tiles_dev, heads, tiles_dev)
    request = jnp.any(wanted, axis=1).reshape(blocks, pair_count).astype(jnp.int32)
    order_num = jnp.cumsum(request, axis=1) - request
    chosen = (order_num[:, None, :] == jnp.arange(capacity, dtype=jnp.int32)[None, :, None]) & (
        request[:, None, :] > 0
    )
    flat_pick = jnp.sum(
        chosen.astype(jnp.int32) * jnp.arange(pair_count, dtype=jnp.int32)[None, None, :], axis=2
    )
    pick_head = flat_pick // tiles_dev
    pick_tile = flat_pick % tiles_dev
    split_keys = keys.reshape(tiles_dev, tile_len, heads, head_dim)
    split_vals = values.reshape(tiles_dev, tile_len, heads, head_dim)
    send_key = split_keys[pick_tile, :, pick_head, :]
    send_val = split_vals[pick_tile, :, pick_head, :]
    recv_key, recv_val = (
        lax.all_to_all(send_key, "seq", split_axis=0, concat_axis=0, tiled=True),
        lax.all_to_all(send_val, "seq", split_axis=0, concat_axis=0, tiled=True),
    )
    own_list = lax.dynamic_slice_in_dim(block_list, device * tiles_dev, tiles_dev, 0)
    own_len = lax.dynamic_slice_in_dim(list_len, device * tiles_dev, tiles_dev, 0)
    own_live = jnp.arange(LIST, dtype=jnp.int32)[None, None, :] < own_len[:, :, None]
    hits = (own_list[..., None] == jnp.arange(tiles_total, dtype=jnp.int32)) & own_live[..., None]
    asked = jnp.any(hits, axis=(0, 2)).reshape(heads, blocks, tiles_dev)
    asked = jnp.transpose(asked, (1, 0, 2)).reshape(blocks, pair_count).astype(jnp.int32)
    slot_table = jnp.cumsum(asked, axis=1) - asked
    source_ids = own_list // tiles_dev
    column_ids = (
        jnp.arange(heads, dtype=jnp.int32)[None, :, None] * tiles_dev + own_list % tiles_dev
    )
    slot_ids = slot_table[source_ids, column_ids]
    scale = 1.0 / math.sqrt(head_dim)

    def head_major(extended):
        moved = extended.reshape(TIME_TILES + 2, ext_cols * tile_len, heads, head_dim)
        return jnp.transpose(moved, (2, 0, 1, 3))

    key_heads = head_major(key_ext)
    val_heads = head_major(val_ext)
    key_windows = jnp.concatenate([key_heads[:, a : a + TIME_TILES] for a in range(3)], axis=2)
    val_windows = jnp.concatenate([val_heads[:, a : a + TIME_TILES] for a in range(3)], axis=2)
    query_heads = jnp.transpose(
        queries.reshape(TIME_TILES, ROW_TILES * tile_len, heads, head_dim), (2, 0, 1, 3)
    )
    far_keys = recv_key[source_ids, slot_ids]
    far_vals = recv_val[source_ids, slot_ids]
    far_key_heads = jnp.transpose(far_keys, (1, 0, 2, 3, 4)).reshape(
        heads, tiles_dev, LIST * tile_len, head_dim
    )
    far_val_heads = jnp.transpose(far_vals, (1, 0, 2, 3, 4)).reshape(
        heads, tiles_dev, LIST * tile_len, head_dim
    )
    far_live = jnp.transpose(own_live, (1, 0, 2))
    span_tiles = 3 * ext_cols

    def one_head(inputs):
        query_one, key_win, val_win, far_key, far_val, reach_time, reach_rows, live_one = inputs
        win_ok = (
            valid_rows[:, None, :, :]
            & (col_gap[None, :, None, :] <= jnp.minimum(reach_rows, 1))
            & (time_gap[None, None, :, None] <= reach_time)
        )
        win_ok = win_ok.reshape(tiles_dev, 1, span_tiles, 1)
        near = (
            jnp.einsum("tqd,tkd->tqk", query_one, key_win, preferred_element_type=jnp.float32)
            * scale
        )
        near = near.reshape(tiles_dev, tile_len, span_tiles, tile_len)
        near = jnp.where(win_ok, near, BIG_NEG).reshape(tiles_dev, tile_len, span_tiles * tile_len)
        query_tiles = query_one.reshape(tiles_dev, tile_len, head_dim)
        far = (
            jnp.einsum("txd,tyd->txy", query_tiles, far_key, preferred_element_type=jnp.float32)
            * scale
        )
        far_ok = jnp.repeat(live_one, tile_len, axis=1)[:, None, :]
        far = jnp.where(far_ok, far, BIG_NEG)
        top = jnp.maximum(jnp.max(near, axis=2, keepdims=True), jnp.max(far, axis=2, keepdims=True))
        near_weights = jnp.exp(near - top)
        far_weights = jnp.exp(far - top)
        total = jnp.sum(near_weights, axis=2, keepdims=True) + jnp.sum(
            far_weights, axis=2, keepdims=True
        )
        near_rounded = near_weights.astype(jnp.bfloat16).reshape(
            TIME_TILES, ROW_TILES * tile_len, span_tiles * tile_len
        )
        mixed = jnp.einsum(
            "tqk,tkd->tqd", near_rounded, val_win, preferred_element_type=jnp.float32
        )
        mixed = mixed.reshape(tiles_dev, tile_len, head_dim)
        mixed = mixed + jnp.einsum(
            "txy,tyd->txd",
            far_weights.astype(jnp.bfloat16),
            far_val,
            preferred_element_type=jnp.float32,
        )
        return (mixed / total).astype(jnp.bfloat16)

    results = lax.map(
        one_head,
        (
            query_heads,
            key_windows,
            val_windows,
            far_key_heads,
            far_val_heads,
            window_time,
            window_rows,
            far_live,
        ),
    )
    return jnp.transpose(results, (1, 2, 0, 3)).reshape(tiles_dev, tile_len, feat)


def solution(mesh):
    return jax.shard_map(
        on_device,
        mesh=mesh,
        in_specs=(
            P(("group", "seq"), None, None),
            P(("group", "seq"), None, None),
            P(("group", "seq"), None, None),
            P("group", None, None),
            P("group", None),
            P(),
            P(),
        ),
        out_specs=P(("group", "seq"), None, None),
        check_vma=False,
    )
```

profile of v0, /device:TPU:1, one launch (start us, length us, event | category | flops | bytes accessed | tf_op | source)
XLA Modules:
  0.0 667.0 jit_solution(11511797322227470170)
XLA Ops:
  0.0 2.4 fusion.30
  2.4 2.2 fusion.31
  5.7 2.3 copy.85
  8.6 2.8 copy.95
  11.5 2.1 gather_fusion
  13.6 7.3 %all-to-all-start = ((bf16[16,4,128,128]{3,2,1,0:T(8,128)(2,1)}), bf16[16,4,128,128]{3,2,1,0:T(8,128)(2,1)}, u32[]{:S(2)}, u32[]{:S(2)}) async-start(bf16[16,4,128,128]{3,2,1,0:T(8,128)(2,1)} %bitcast.205), calls=%async_computation | async-start | bytes 4194304 | tf_op jit(solution)/shard_map/all_to_all | solution.py:115
  26.6 4.8 collective-permute-start.4
  35.6 3.5 scatter.26
  39.1 3.9 copy.109
  43.3 4.0 copy.110
  47.3 3.7 gather_fusion.3
  51.1 4.4 reshape.609
  55.5 3.5 copy.111
  61.9 5.5 collective-permute-start.1
  67.6 4.5 scatter.39
  72.1 4.6 scatter.31
  78.0 134.6 %collective-permute-done.4 = bf16[1,4,128,2560]{3,2,1,0:T(8,128)(2,1)} collective-permute-done((bf16[1,4,128,2560]{3,2,1,0:T(8,128)(2,1)}, bf16[1,4,128,2560]{3,2,1,0:T(8,128)(2,1)}, u32[]{:S(2)}, u32[]{:S(2)}) %collective-permute-start.4) | collective-permute-done | bytes 2621472 | tf_op jit(solution)/shard_map/ppermute | solution.py:30
  212.6 3.5 constant_dynamic-update-slice_fusion.2
  216.1 6.8 %all-to-all-start.1 = ((bf16[16,4,128,128]{3,2,1,0:T(8,128)(2,1)}), bf16[16,4,128,128]{3,2,1,0:T(8,128)(2,1)S(1)}, u32[]{:S(2)}, u32[]{:S(2)}) async-start(bf16[16,4,128,128]{3,2,1,0:T(8,128)(2,1)} %bitcast.206), calls=%async_computation.1 | async-start | bytes 4194304 | tf_op jit(solution)/shard_map/all_to_all | solution.py:116
  222.9 3.4 constant_dynamic-update-slice_fusion.1
  226.3 17.1 %reshape.620 = bf16[3,640,20,128]{3,2,1,0:T(8,128)(2,1)} reshape(bf16[3,5,128,2560]{3,2,1,0:T(8,128)(2,1)} %constant_dynamic-update-slice_fusion.1) | data formatting | bytes 19660800 | tf_op jit(solution)/shard_map/reshape | solution.py:133
  243.5 5.5 fusion.55
  248.9 60.3 %pad_maximum_fusion.1 = bf16[20,1,1920,128]{3,0,2,1:T(8,128)(2,1)} fusion(bf16[20,1,640,128]{3,0,2,1:T(8,128)(2,1)S(1)} %get-tuple-element.260, bf16[20,1,640,128]{3,0,2,1:T(8,128)(2,1)S(1)} %get-tuple-element.261, bf16[20,1,640,128]{3,0,2,1:T(8,128)(2,1)S(1)} %get-tuple-element.259), kind=kLoop, calls=%fused_computation.50 | loop fusion | flops 9830400 | bytes 19660800 | tf_op jit(solution)/shard_map/concatenate | solution.py:139
  309.2 10.1 %copy.114 = bf16[20,1,1920,128]{3,2,1,0:T(8,128)(2,1)} copy(bf16[20,1,1920,128]{3,0,2,1:T(8,128)(2,1)} %pad_maximum_fusion.1) | data formatting | bytes 19660800
  319.3 3.4 constant_dynamic-update-slice_fusion.4
  322.7 3.5 constant_dynamic-update-slice_fusion.3
  326.3 17.1 %reshape.613 = bf16[3,640,20,128]{3,2,1,0:T(8,128)(2,1)} reshape(bf16[3,5,128,2560]{3,2,1,0:T(8,128)(2,1)} %constant_dynamic-update-slice_fusion.3) | data formatting | bytes 19660800 | tf_op jit(solution)/shard_map/reshape | solution.py:133
  343.4 5.5 fusion.56
  348.9 60.3 %pad_maximum_fusion = bf16[20,1,1920,128]{3,0,2,1:T(8,128)(2,1)} fusion(bf16[20,1,640,128]{3,0,2,1:T(8,128)(2,1)S(1)} %get-tuple-element.263, bf16[20,1,640,128]{3,0,2,1:T(8,128)(2,1)S(1)} %get-tuple-element.264, bf16[20,1,640,128]{3,0,2,1:T(8,128)(2,1)S(1)} %get-tuple-element.262), kind=kLoop, calls=%fused_computation.49 | loop fusion | flops 9830400 | bytes 19660800 | tf_op jit(solution)/shard_map/concatenate | solution.py:138
  409.2 10.2 %copy.112 = bf16[20,1,1920,128]{3,2,1,0:T(8,128)(2,1)} copy(bf16[20,1,1920,128]{3,0,2,1:T(8,128)(2,1)} %pad_maximum_fusion) | data formatting | bytes 19660800
  419.4 4.9 gather_fusion.2
  424.3 3.3 gather_fusion.4
  427.6 235.0 %while.20 = (s32[]{:T(128)}, bf16[20,3,128,128]{2,3,0,1:T(8,128)(2,1)}, pred[1,3,5]{2,1,0:T(4,128)(4,1)}, s32[20]{0:T(128)S(1)}, s32[20]{0:T(128)S(1)}, /*index=...) while((s32[]{:T(128)}, ...), condition=%wide.wide.region_11.12_spmd.clone, body=%wide.wide.region_6.11_spmd.clone.sunk | while | flops 433078048 | bytes 14210132 | solution.py:196
  430.7 1.8 fusion.89
  442.5 1.8 fusion.89
  454.2 1.8 fusion.89
  466.0 1.8 fusion.89
  489.5 1.8 fusion.89
  513.0 1.8 fusion.89
  536.5 1.8 fusion.89
  548.2 1.8 fusion.89
  583.5 1.8 fusion.89
  595.3 1.8 fusion.89
  607.0 1.8 fusion.89
  630.5 1.8 fusion.89
  642.3 1.8 fusion.89
  654.0 1.8 fusion.89
  662.6 4.0 copy.117
  (613 shorter events, 211.4 us)
Async XLA Ops:
  0.0 5.7 copy-start.1
  0.0 5.1 copy-start.3
  0.0 5.1 copy-start.2
  2.4 21.1 %collective-permute-start.3 = (bf16[1,128,2560]{2,1,0:T(8,128)(2,1)}, bf16[1,128,2560]{2,1,0:T(8,128)(2,1)}, u32[]{:S(2)}, u32[]{:S(2)}) collective-permute-start(bf16[1,128,2560]{2,1,0:T(8,128)(2,1)} %fusion.30), channel_id=1, source_target_pairs={{0,1},{1,0},{2,3},{3,2},{4,5},{5,4},{6,7},{7,6},{8,9},{9,8},{10,11... | collective-permute-start | bytes 1966088 | tf_op jit(solution)/shard_map/ppermute | solution.py:24
  4.6 54.4 %collective-permute-start = (bf16[1,128,2560]{2,1,0:T(8,128)(2,1)}, bf16[1,128,2560]{2,1,0:T(8,128)(2,1)}, u32[]{:S(2)}, u32[]{:S(2)}) collective-permute-start(bf16[1,128,2560]{2,1,0:T(8,128)(2,1)} %fusion.31), channel_id=1, source_target_pairs={{0,1},{1,0},{2,3},{3,2},{4,5},{5,4},{6,7},{7,6},{8,9},{9,8},{10,11... | collective-permute-start | bytes 1966088 | tf_op jit(solution)/shard_map/ppermute | solution.py:24
  13.6 202.6 %all-to-all-start = ((bf16[16,4,128,128]{3,2,1,0:T(8,128)(2,1)}), bf16[16,4,128,128]{3,2,1,0:T(8,128)(2,1)}, u32[]{:S(2)}, u32[]{:S(2)}) async-start(bf16[16,4,128,128]{3,2,1,0:T(8,128)(2,1)} %bitcast.205), calls=%async_computation | async-start | bytes 4194304 | tf_op jit(solution)/shard_map/all_to_all | solution.py:115
  26.6 186.0 %collective-permute-start.4 = (bf16[1,4,128,2560]{3,2,1,0:T(8,128)(2,1)}, bf16[1,4,128,2560]{3,2,1,0:T(8,128)(2,1)}, u32[]{:S(2)}, u32[]{:S(2)}) collective-permute-start(bf16[1,4,128,2560]{3,2,1,0:T(8,128)(2,1)} %constant_dynamic-slice_fusion.3), channel_id=1, source_target_pairs={{0,2},{1,3},{2,4},{3,5},{4,6},{5,7},{6,8},{7,9},{8,10},{9,11},{10,... | collective-permute-start | bytes 7864328 | tf_op jit(solution)/shard_map/ppermute | solution.py:30
  34.3 188.7 %collective-permute-start.5 = (bf16[1,4,128,2560]{3,2,1,0:T(8,128)(2,1)}, bf16[1,4,128,2560]{3,2,1,0:T(8,128)(2,1)}, u32[]{:S(2)}, u32[]{:S(2)}) collective-permute-start(bf16[1,4,128,2560]{3,2,1,0:T(8,128)(2,1)} %constant_dynamic-slice_fusion.3), channel_id=1, source_target_pairs={{2,0},{3,1},{4,2},{5,3},{6,4},{7,5},{8,6},{9,7},{10,8},{11,9},{12,... | collective-permute-start | bytes 7864328 | tf_op jit(solution)/shard_map/ppermute | solution.py:30
  35.6 15.4 %copy-start.4 = (pred[1,3,5]{2,1,0:T(4,128)(4,1)}, pred[1,3,5]{2,1,0:T(4,128)(4,1)S(1)}, u32[]{:S(2)}) copy-start(pred[1,3,5]{2,1,0:T(4,128)(4,1)S(1)} %pad_add_fusion) | copy-start | bytes 49
  55.5 3.5 copy-start
  61.9 257.4 %collective-permute-start.1 = (bf16[1,4,128,2560]{3,2,1,0:T(8,128)(2,1)}, bf16[1,4,128,2560]{3,2,1,0:T(8,128)(2,1)}, u32[]{:S(2)}, u32[]{:S(2)}) collective-permute-start(bf16[1,4,128,2560]{3,2,1,0:T(8,128)(2,1)} %constant_dynamic-slice_fusion.6), channel_id=1, source_target_pairs={{0,2},{1,3},{2,4},{3,5},{4,6},{5,7},{6,8},{7,9},{8,10},{9,11},{10,... | collective-permute-start | bytes 7864328 | tf_op jit(solution)/shard_map/ppermute | solution.py:30
  76.7 246.0 %collective-permute-start.2 = (bf16[1,4,128,2560]{3,2,1,0:T(8,128)(2,1)}, bf16[1,4,128,2560]{3,2,1,0:T(8,128)(2,1)}, u32[]{:S(2)}, u32[]{:S(2)}) collective-permute-start(bf16[1,4,128,2560]{3,2,1,0:T(8,128)(2,1)} %constant_dynamic-slice_fusion.6), channel_id=1, source_target_pairs={{2,0},{3,1},{4,2},{5,3},{6,4},{7,5},{8,6},{9,7},{10,8},{11,9},{12,... | collective-permute-start | bytes 7864328 | tf_op jit(solution)/shard_map/ppermute | solution.py:30
  216.1 208.2 %all-to-all-start.1 = ((bf16[16,4,128,128]{3,2,1,0:T(8,128)(2,1)}), bf16[16,4,128,128]{3,2,1,0:T(8,128)(2,1)S(1)}, u32[]{:S(2)}, u32[]{:S(2)}) async-start(bf16[16,4,128,128]{3,2,1,0:T(8,128)(2,1)} %bitcast.206), calls=%async_computation.1 | async-start | bytes 4194304 | tf_op jit(solution)/shard_map/all_to_all | solution.py:116
  424.3 3.3 copy-start.5
  424.3 3.3 copy-start.6
where the time goes:
time: 678 us; the launch traced here: 667 us
  local copies, waits for them, and re-layouts  214 us (32%)
  other arithmetic  159 us (23%)
  waiting for transfers between devices  135 us (20%)
  matrix products  118 us (17%)
  starting transfers between devices  27.5 us (4%)
  loops' own time  14 us (2%)
    ppermute x4, waiting for transfers between devices, passed_along(): lax.ppermute(value, axis, [(source, source + steps) for source in range(i...  135 us
    concatenate x1, other arithmetic, on_device(): jnp.concatenate([key_heads[:, a:a + TIME_TILES] for a in range(3)], axis=2)  60.3 us
    concatenate x1, other arithmetic, on_device(): jnp.concatenate([val_heads[:, a:a + TIME_TILES] for a in range(3)], axis=2)  60.3 us
    dynamic_slice x60, local copies, waits for them, and re-layouts, on_device(): lax.map(one_head, (query_heads, key_windows, val_windows, far_key_heads,...  43.6 us
    dot_general x20, matrix products, one_head(): jnp.einsum('tqd,tkd->tqk', query_one, key_win, preferred_element_type=jnp...  36.9 us
    reshape x2, local copies, waits for them, and re-layouts, head_major(): extended.reshape(TIME_TILES + 2, ext_cols * tile_len, heads, head_dim)  34.3 us
    dot_general x20, matrix products, one_head(): jnp.einsum('tqk,tkd->tqd', near_rounded, val_win, preferred_element_type=...  31.7 us
    unnamed x19, local copies, waits for them, and re-layouts  30 us
  transfers between devices with their start and end apart: 8, of which 1 were waited for; matrix products, arithmetic and copies ran while one was open for 39% of the time, Pallas kernels for 0%

commit v1 on v0

v1 whole, which is shorter than its diff:
```python
import functools
import math

import jax
import jax.numpy as jnp
from jax import lax
from jax.experimental import pallas as pl
from jax.experimental.pallas import tpu as pltpu
from jax.sharding import PartitionSpec as P


ROW_BLOCKS = 2
LIST = 2
BIG_NEG = -1e30
BIG_INT = 1 << 20

CAPS = (7, 9, 11, 13)


def relay_fits(mesh):
    where = mesh.devices[0]
    chips = [getattr(dev, "coords", None) for dev in where[::ROW_BLOCKS]]
    if any(c is None for c in chips) or len(chips) % 2:
        return False

    def gap(a, b):
        return sum(abs(p - q) for p, q in zip(chips[a], chips[b]))

    count = len(chips)
    return (
        all(gap(t, t + 1) == 1 for t in range(0, count, 2))
        and all(gap(t, t + 1) == 2 for t in range(1, count - 1, 2))
        and all(gap(t, t + 2) == 1 for t in range(count - 2))
    )


def column(head, width):
    return pl.ds(pl.multiple_of(head * width, width), width)


def pack_kernel(
    timed, device, lists, lens, lists_s, lens_s, key_hbm, val_hbm,
    halo_key, halo_val, edge, far, plan, kbuf, vbuf, span, words, code, sem_in, sem_out, sem_code
):
    heads = timed.shape[0]
    tiles = kbuf.shape[0]
    cap = halo_key.shape[0]
    blocks, _, slots, _, width = far.shape
    me = device[0]
    base = me * tiles
    loads = [
        pltpu.make_async_copy(key_hbm, kbuf, sem_in.at[0]),
        pltpu.make_async_copy(val_hbm, vbuf, sem_in.at[1]),
    ]
    for load in loads:
        load.start()

    span[...] = jnp.zeros_like(span)
    low = high = None
    for entry in range(LIST):
        live = lens[...] > entry
        item = lists[:, entry, :]
        small, large = jnp.where(live, item, BIG_INT), jnp.where(live, item, -1)
        low = small if low is None else jnp.minimum(low, small)
        high = large if high is None else jnp.maximum(high, large)
    span[0, :heads, : low.shape[1]] = low
    span[1, :heads, : low.shape[1]] = high
    lanes = span.shape[2]
    low = low_in = span[0]
    high = high_in = span[1]
    for u in range(1, tiles):
        low = jnp.minimum(low, pltpu.roll(low_in, lanes - u, 1))
        high = jnp.maximum(high, pltpu.roll(high_in, lanes - u, 1))
    rows = lax.broadcasted_iota(jnp.int32, low.shape, 0)
    want = (low >= base) & (low < base + tiles) & (rows < heads)
    count = low.shape[0]
    under = lax.broadcasted_iota(jnp.int32, (count, count), 1) < lax.broadcasted_iota(
        jnp.int32, (count, count), 0
    )
    order = jnp.dot(
        jnp.where(under, 1.0, 0.0), jnp.where(want, 1.0, 0.0), preferred_element_type=jnp.float32
    )
    word = rows * 16 + (low - base) * 4 + (high - base)
    for r in range(slots // LIST):
        chosen = want & (order > r - 0.5) & (order < r + 0.5)
        words[r : r + 1, :] = jnp.sum(jnp.where(chosen, word, 0), axis=0, keepdims=True)
    to_scalar = pltpu.make_async_copy(words, code, sem_code)
    to_scalar.start()

    def note(h, found):
        @pl.when(timed[h] > 0)
        def _():
            plan[3, found] = h

        return found + jnp.where(timed[h] > 0, 1, 0)

    found = lax.fori_loop(0, heads, note, jnp.int32(0))
    plan[4, 0] = found
    last = jnp.where(found > 0, plan[3, jnp.maximum(found - 1, 0)], 0)

    @pl.loop(0, cap)
    def _(slot):
        @pl.when(slot >= found)
        def _():
            plan[3, slot] = last

    side = jnp.where(me % ROW_BLOCKS == 0, tiles - 1, 0)
    bufs = (kbuf, vbuf)
    for part, halo in enumerate((halo_key, halo_val)):
        loads[part].wait()
        pltpu.make_async_copy(bufs[part].at[side], edge.at[part], sem_out.at[2]).start()

        @pl.loop(0, cap)
        def _(slot):
            pltpu.make_async_copy(
                bufs[part].at[:, :, column(plan[3, slot], width)], halo.at[slot], sem_out.at[part]
            ).start()

    to_scalar.wait()

    @pl.loop(0, blocks)
    def _(dest):
        for r in range(slots // LIST):
            item = code[r, dest * tiles]
            for part in range(2):
                for which, tile in enumerate((item // 4 % 4, item % 4)):
                    pltpu.make_async_copy(
                        bufs[part].at[tile, :, column(item // 16, width)],
                        far.at[dest, part, r * LIST + which],
                        sem_out.at[3],
                    ).start()

    @pl.loop(0, blocks)
    def _(b):
        plan[5, b] = 0

    @pl.loop(0, heads)
    def _(h):
        small = jnp.int32(BIG_INT)
        large = jnp.int32(-1)
        got = []
        for u in range(tiles):
            for entry in range(LIST):
                live = lens_s[h, base + u] > entry
                item = jnp.where(live, lists_s[h, entry, base + u], -1)
                got.append((u, item))
                small = jnp.where(live, jnp.minimum(small, item), small)
                large = jnp.maximum(large, item)
        bits = jnp.int32(0)
        for u, item in got:
            bits |= jnp.where(item == small, 1 << (u * LIST), 0)
            bits |= jnp.where(item == large, 2 << (u * LIST), 0)
        owner = small // tiles
        plan[0, h] = owner
        plan[1, h] = plan[5, owner]
        plan[2, h] = bits
        plan[5, owner] = plan[5, owner] + 1

    pltpu.make_async_copy(halo_key, halo_key, sem_out.at[0]).wait()
    pltpu.make_async_copy(halo_val, halo_val, sem_out.at[1]).wait()
    pltpu.make_async_copy(edge, edge, sem_out.at[2]).wait()
    pltpu.make_async_copy(far, far, sem_out.at[3]).wait()


def scores_of(query, keys):
    return lax.dot_general(
        query, keys, (((1,), (1,)), ((), ())), preferred_element_type=jnp.float32
    )


def with_ones(vals):
    return jnp.concatenate([vals, jnp.ones_like(vals)], axis=1)


def around(u, rows):
    return [u] if not rows else [u - 1, u, u + 1]


def softmax_step(blocks, vals, old, factor):
    width = vals.shape[1]
    top = jnp.max(functools.reduce(jnp.maximum, blocks), axis=1, keepdims=True)
    if old is not None:
        top = jnp.maximum(old[1], top)
    else:
        top = jnp.broadcast_to(top, (blocks[0].shape[0], width))
    shift = top * factor
    weights = [jnp.exp2(block * factor - shift).astype(jnp.bfloat16) for block in blocks]
    both = jnp.dot(
        jnp.concatenate(weights, axis=1), with_ones(vals), preferred_element_type=jnp.float32
    )
    mixed, total = both[:, :width], both[:, width:]
    if old is not None:
        keep = jnp.exp2(old[1] * factor - shift)
        mixed = old[0] * keep + mixed
        total = old[2] * keep + total
    return mixed, top, total


def window_kernel(keys, vals, edge_key, edge_val, q_ref, old, new, rows, row_pos, factor):
    tiles, tile_len, _ = q_ref.shape
    neg, zero = jnp.float32(BIG_NEG), jnp.float32(0)
    for u in range(tiles):
        pieces = []
        for w in around(u, rows):
            if 0 <= w < tiles:
                pieces.append((keys(w), vals(w), None))
            else:
                on = row_pos == (1 if w < 0 else 0)
                pieces.append((edge_key(), edge_val(), jnp.where(on, zero, neg)))
        raw = scores_of(q_ref[u], jnp.concatenate([p[0] for p in pieces], axis=0))
        blocks = []
        for at, (_, _, bias) in enumerate(pieces):
            block = raw[:, at * tile_len : (at + 1) * tile_len]
            blocks.append(block if bias is None else block + bias)
        state = None if old is None else [ref[u] for ref in old]
        result = softmax_step(
            blocks, jnp.concatenate([p[1] for p in pieces], axis=0), state, factor
        )
        for ref, value in zip(new, result):
            ref[u] = value


def local_kernel(reach, device, q_ref, k_ref, v_ref, edge_ref, *new, factor):
    head = pl.program_id(0)
    row_pos = device[0] % ROW_BLOCKS
    for rows in (0, 1):

        @pl.when((reach[head] > 0) == bool(rows))
        def _():
            window_kernel(
                lambda w: k_ref[w],
                lambda w: v_ref[w],
                lambda: edge_ref[0],
                lambda: edge_ref[1],
                q_ref, None, new, rows, row_pos, factor,
            )


def time_kernel(
    plan, reach, device, valid, q_ref, k_ref, v_ref, edge_ref, *refs, factor
):
    old, new = refs[:3], refs[3:]
    slot = pl.program_id(0)
    head = plan[3, slot]
    row_pos = device[0] % ROW_BLOCKS
    go = (slot < plan[4, 0]) & (valid[0] > 0)
    for rows in (0, 1):

        @pl.when(go & ((reach[head] > 0) == bool(rows)))
        def _():
            window_kernel(
                lambda w: k_ref[0, w],
                lambda w: v_ref[0, w],
                lambda: edge_ref[0, 0],
                lambda: edge_ref[1, 0],
                q_ref, old, new, rows, row_pos, factor,
            )

    @pl.when((slot < plan[4, 0]) & (valid[0] == 0) | (slot == 0) & (plan[4, 0] == 0))
    def _():
        for before, after in zip(old, new):
            after[...] = before[...]


def far_kernel(plan, q_ref, acc_ref, top_ref, sum_ref, *refs, factor):
    fars, out_ref = refs[:-1], refs[-1]
    step = pl.program_id(0)
    tiles, tile_len, _ = q_ref.shape
    width = fars[0].shape[-1]
    neg, zero = jnp.float32(BIG_NEG), jnp.float32(0)
    for g, far_ref in enumerate(fars):
        at = slice(g * width, (g + 1) * width)
        word = plan[2, step * len(fars) + g]
        keys = far_ref[0, 0].reshape(LIST * tile_len, width)
        vals = far_ref[0, 1].reshape(LIST * tile_len, width)
        for u in range(tiles):
            raw = scores_of(q_ref[u, :, at], keys)
            blocks = []
            for which in range(LIST):
                live = (word // (1 << (u * LIST + which))) % 2
                block = raw[:, which * tile_len : (which + 1) * tile_len]
                blocks.append(block + jnp.where(live > 0, zero, neg))
            state = (acc_ref[u, :, at], top_ref[u, :, at], sum_ref[u, :, at])
            mixed, _, total = softmax_step(blocks, vals, state, factor)
            out_ref[u, :, at] = (mixed / total).astype(out_ref.dtype)


def any_spec():
    return pl.BlockSpec(memory_space=pl.ANY)


def smem_spec():
    return pl.BlockSpec(memory_space=pltpu.SMEM)


def vmem_spec():
    return pl.BlockSpec(memory_space=pltpu.VMEM)


def on_device(relay, queries, keys, values, block_list, list_len, window_time, window_rows):
    tiles, tile_len, feat = queries.shape
    heads = window_time.shape[0]
    width = feat // heads
    blocks = lax.axis_size("seq")
    axis = lax.axis_index("seq").astype(jnp.int32)
    device = axis.reshape(1)
    time_block = axis // ROW_BLOCKS
    row_pos = axis % ROW_BLOCKS
    time_blocks = blocks // ROW_BLOCKS
    dtype = keys.dtype
    factor = math.log2(math.e) / math.sqrt(width)
    timed_count = jnp.sum((window_time > 0).astype(jnp.int32))
    side = jnp.where(row_pos == 0, tiles - 1, 0)
    if relay:
        first_ok = jnp.int32(1)
        second_ok = jnp.where(time_block % 2 == 0, time_block > 0, time_block < time_blocks - 1)
    else:
        first_ok = time_block > 0
        second_ok = time_block < time_blocks - 1
    oks = [ok.astype(jnp.int32).reshape(1) for ok in (first_ok, second_ok)]
    lists = jnp.transpose(block_list, (1, 2, 0))
    lens = jnp.transpose(list_len, (1, 0))
    per_source = (heads + blocks - 2) // (blocks - 1)
    slots = per_source * LIST
    pair_tile = tile_len * width * 2
    lanes = -(-lists.shape[2] // 128) * 128
    sublanes = -(-heads // 8) * 8
    pair_route = [(i, i ^ 1) for i in range(blocks)]

    def permute(value, route):
        return lax.ppermute(value, "seq", route)

    def at_head(h, *_):
        return (0, 0, h)

    state_shape = [jax.ShapeDtypeStruct((tiles, tile_len, feat), jnp.float32)] * 3
    tile_spec = pl.BlockSpec((tiles, tile_len, width), at_head)

    def near(cap):
        return near_of(cap)

    def near_of(cap):
        halo_shape = jax.ShapeDtypeStruct((cap, tiles, tile_len, width), dtype)
        halo_key, halo_val, edge, far, plan = pl.pallas_call(
            pack_kernel,
            out_shape=(
                halo_shape,
                halo_shape,
                jax.ShapeDtypeStruct((2, tile_len, feat), dtype),
                jax.ShapeDtypeStruct((blocks, 2, slots, tile_len, width), dtype),
                jax.ShapeDtypeStruct((8, 128), jnp.int32),
            ),
            in_specs=[smem_spec(), smem_spec(), vmem_spec(), vmem_spec(), smem_spec(), smem_spec()]
            + [any_spec()] * 2,
            out_specs=[any_spec()] * 4 + [smem_spec()],
            scratch_shapes=[
                pltpu.VMEM(keys.shape, dtype),
                pltpu.VMEM(values.shape, dtype),
                pltpu.VMEM((2, sublanes, lanes), jnp.int32),
                pltpu.VMEM((8, lanes), jnp.int32),
                pltpu.SMEM((8, lanes), jnp.int32),
                pltpu.SemaphoreType.DMA((2,)),
                pltpu.SemaphoreType.DMA((4,)),
                pltpu.SemaphoreType.DMA,
            ],
            cost_estimate=pl.CostEstimate(
                flops=0,
                transcendentals=0,
                bytes_accessed=(2 * blocks * slots + 6 * cap) * pair_tile,
            ),
            name="pack",
        )(window_time, device, lists, lens, lists, lens, keys, values)

        if relay:
            step = 2 * ROW_BLOCKS
            one_hop = [(i, i ^ ROW_BLOCKS) for i in range(blocks)]
            other = []
            for i in range(blocks):
                to = i + step if (i // ROW_BLOCKS) % 2 == 0 else i - step
                if 0 <= to < blocks:
                    other.append((i, to))
            straight = []
            for i in range(blocks):
                to = i - ROW_BLOCKS if (i // ROW_BLOCKS) % 2 == 0 else i + ROW_BLOCKS
                if 0 <= to < blocks:
                    straight.append((i, to))
            first_key = permute(halo_key, one_hop)
            first_val = permute(halo_val, one_hop)
            first = [first_key, first_val]
            second_key = permute(first_key, other)
            second_val = permute(halo_val, straight)
            second = [second_key, second_val]
        else:
            step = ROW_BLOCKS
            after = [(i, i + step) for i in range(blocks - step)]
            ahead = [(i + step, i) for i in range(blocks - step)]
            first_key = permute(halo_key, after)
            first_val = permute(halo_val, after)
            first = [first_key, first_val]
            second_key = permute(halo_key, ahead)
            second_val = permute(halo_val, ahead)
            second = [second_key, second_val]
        far = lax.all_to_all(far, "seq", split_axis=0, concat_axis=0, tiled=True)
        edge = permute(edge, pair_route)

        pairs = heads * tiles * 3
        state = pl.pallas_call(
            functools.partial(local_kernel, factor=factor),
            grid_spec=pltpu.PrefetchScalarGridSpec(
                num_scalar_prefetch=2,
                grid=(heads,),
                in_specs=[tile_spec] * 3 + [pl.BlockSpec((2, tile_len, width), at_head)],
                out_specs=[tile_spec] * 3,
            ),
            out_shape=state_shape,
            cost_estimate=pl.CostEstimate(
                flops=pairs * 4 * tile_len * tile_len * width,
                transcendentals=pairs * tile_len * tile_len,
                bytes_accessed=10 * tiles * tile_len * feat * 2,
            ),
            name="local",
        )(window_rows, device, queries, keys, values, edge)

        def at_plan(s, plan_ref, *_):
            return (0, 0, plan_ref[3, s])

        planned = pl.BlockSpec((tiles, tile_len, width), at_plan)
        pairs = cap * tiles * 3
        for halo, ok in zip((first, second), oks):
            sides = jnp.stack([lax.dynamic_index_in_dim(x, side, 1, keepdims=False) for x in halo])
            sides = permute(sides, pair_route)
            halo_spec = pl.BlockSpec((1, tiles, tile_len, width), lambda s, *_: (s, 0, 0, 0))
            state = pl.pallas_call(
                functools.partial(time_kernel, factor=factor),
                grid_spec=pltpu.PrefetchScalarGridSpec(
                    num_scalar_prefetch=4,
                    grid=(cap,),
                    in_specs=[
                        planned,
                        halo_spec,
                        halo_spec,
                        pl.BlockSpec((2, 1, tile_len, width), lambda s, *_: (0, s, 0, 0)),
                        planned,
                        planned,
                        planned,
                    ],
                    out_specs=[planned] * 3,
                ),
                out_shape=state_shape,
                input_output_aliases={8: 0, 9: 1, 10: 2},
                cost_estimate=pl.CostEstimate(
                    flops=pairs * 4 * tile_len * tile_len * width,
                    transcendentals=pairs * tile_len * tile_len,
                    bytes_accessed=16 * cap * tiles * pair_tile,
                ),
                name="time",
            )(plan, window_rows, device, ok, queries, halo[0], halo[1], sides, *state)
        return (*state, far, plan)

    caps = [c for c in CAPS if c < heads] + [heads]
    pick = sum((timed_count > c).astype(jnp.int32) for c in caps[:-1])
    *state, far, plan = lax.switch(pick, [functools.partial(near, c) for c in caps])

    group = 2 if heads % 2 == 0 else 1
    wide_spec = pl.BlockSpec((tiles, tile_len, width * group), at_head)

    def far_spec(g):
        return pl.BlockSpec(
            (1, 2, LIST, tile_len, width),
            lambda h, plan_ref: (plan_ref[0, h * group + g], 0, plan_ref[1, h * group + g], 0, 0),
        )

    return pl.pallas_call(
        functools.partial(far_kernel, factor=factor),
        grid_spec=pltpu.PrefetchScalarGridSpec(
            num_scalar_prefetch=1,
            grid=(heads // group,),
            in_specs=[wide_spec] * 4 + [far_spec(g) for g in range(group)],
            out_specs=wide_spec,
        ),
        out_shape=jax.ShapeDtypeStruct(queries.shape, queries.dtype),
        cost_estimate=pl.CostEstimate(
            flops=heads * tiles * LIST * 4 * tile_len * tile_len * width,
            transcendentals=heads * tiles * LIST * tile_len * tile_len,
            bytes_accessed=10 * tiles * tile_len * feat * 2,
        ),
        name="far",
    )(plan, queries, *state, *([far] * group))


def solution(mesh):
    return jax.shard_map(
            functools.partial(on_device, relay_fits(mesh)),
            mesh=mesh,
            in_specs=(
                P(("group", "seq"), None, None),
                P(("group", "seq"), None, None),
                P(("group", "seq"), None, None),
                P("group", None, None),
                P("group", None),
                P(),
                P(),
            ),
            out_specs=P(("group", "seq"), None, None),
            check_vma=False,
    )
```

time: 678 us -> 203 us (0.30)
  the two profiles are of different devices: /device:TPU:1 before, /device:TPU:13 now
where the time goes in v1:
time: 203 us; the launch traced here: 201 us
  waiting for transfers between devices  82.1 us (40%)
  Pallas kernels  68.1 us (34%)
  starting transfers between devices  41.8 us (21%)
  other arithmetic  3.16 us (2%)
  local copies, waits for them, and re-layouts  3.07 us (2%)
  between operations  2.61 us (1%)
    ppermute x7, waiting for transfers between devices, permute(): return lax.ppermute(value, 'seq', route)  82.1 us
    ppermute x7, starting transfers between devices, permute(): return lax.ppermute(value, 'seq', route)  35.3 us
    pallas_call x2, Pallas kernels, near_of(): pl.pallas_call(functools.partial(time_kernel, factor=factor), grid_spec=p...  27.5 us
    pallas_call x1, Pallas kernels, near_of(): pl.pallas_call(functools.partial(local_kernel, factor=factor), grid_spec=...  21.3 us
    pallas_call x1, Pallas kernels, on_device(): pl.pallas_call(functools.partial(far_kernel, factor=factor), grid_spec=pl...  12.7 us
    pallas_call x1, Pallas kernels, near_of(): pl.pallas_call(pack_kernel, out_shape=(halo_shape, halo_shape, jax.ShapeD...  6.56 us
    all_to_all x1, starting transfers between devices, near_of(): far = lax.all_to_all(far, 'seq', split_axis=0, concat_axis=0, tiled=True)  6.53 us
  transfers between devices with their start and end apart: 8, of which 3 were waited for; matrix products, arithmetic and copies ran while one was open for 2% of the time, Pallas kernels for 24%

profile of v1, /device:TPU:13, one launch (start us, length us, event | category | flops | bytes accessed | tf_op | source)
XLA Modules:
  0.0 201.4 jit_solution(11288733592367338384)
XLA Ops:
  0.0 1.3 fusion
  3.9 184.8 %conditional.1 = (f32[3,128,2560]{2,1,0:T(8,128)}, f32[3,128,2560]{2,1,0:T(8,128)}, f32[3,128,2560]{2,1,0:T(8,128)}, bf16[16,2,4,128,128]{4,3,2,1,0:T(8,128)(2,1)}, s32[8,128]{1,0:T(8,128)}) conditional(s32[]{:T(128)} %clamp.3, (s32[20]{0:T(128)}, s32[1]{0:T(128)}, s32[20,2,48]{2,1,0:T(2,128)}, s32[20,48]{1,0:T(8,128)}, ...), branch_computations={%region_1.2_spmd, %region_2.3_spmd, %region_3.4_spmd, %region_4.5_... | conditional | flops 4531159040 | bytes 181928768 | solution.py:462
  3.9 6.6 %pack.7 = (bf16[11,3,128,128]{3,2,1,0:T(8,128)(2,1)}, bf16[11,3,128,128]{3,2,1,0:T(8,128)(2,1)}, bf16[2,128,2560]{2,1,0:T(8,128)(2,1)}, bf16[16,2,4,128,128]{4,3,2,1,0:T(8,128)(2,1)}, s32[8,128]{1,0:T(8,128)}) custom-call(s32[20]{0:T(128)} %get-tuple-element.153.timed, s32[1]{0:T(128)} %get-tuple-element.154.device, ...), custom_call_target="tpu_custom_call" | custom-call | bytes 6356992 | tf_op jit(solution)/shard_map/cond/branch_2_fun/pack/pallas_call | solution.py:344
  10.5 6.5 %all-to-all-start.2 = ((bf16[16,2,4,128,128]{4,3,2,1,0:T(8,128)(2,1)}), bf16[16,2,4,128,128]{4,3,2,1,0:T(8,128)(2,1)}, u32[]{:S(2)}, u32[]{:S(2)}) async-start(bf16[16,2,4,128,128]{4,3,2,1,0:T(8,128)(2,1)} %get-tuple-element.176), calls=%async_computation.2 | async-start | bytes 8388608 | tf_op jit(solution)/shard_map/cond/branch_2_fun/all_to_all | solution.py:403
  17.0 0.0 copy-start.2
  17.0 0.0 copy-start.14
  17.0 0.3 collective-permute-start.14
  17.4 1.2 collective-permute-start.18
  18.6 3.1 %collective-permute-start.16 = (bf16[11,3,128,128]{3,2,1,0:T(8,128)(2,1)}, bf16[11,3,128,128]{3,2,1,0:T(8,128)(2,1)S(1)}, u32[]{:S(2)}, u32[]{:S(2)}) collective-permute-start(bf16[11,3,128,128]{3,2,1,0:T(8,128)(2,1)} %get-tuple-element.164), channel_id=1, source_target_pairs={{2,4},{3,5},{4,2},{5,3},{6,8},{7,9},{8,6},{9,7},{10,12},{11,13},{1... | collective-permute-start | bytes 3244040 | tf_op jit(solution)/shard_map/cond/branch_2_fun/ppermute | solution.py:331
  21.7 48.0 %collective-permute-done.14.k_ref = bf16[11,3,128,128]{3,2,1,0:T(8,128)(2,1)} collective-permute-done((bf16[11,3,128,128]{3,2,1,0:T(8,128)(2,1)}, bf16[11,3,128,128]{3,2,1,0:T(8,128)(2,1)}, u32[]{:S(2)}, u32[]{:S(2)}) %collective-permute-start.14) | collective-permute-done | bytes 1081376 | tf_op jit(solution)/shard_map/cond/branch_2_fun/ppermute | solution.py:331
  69.6 26.1 %collective-permute-start.15 = (bf16[11,3,128,128]{3,2,1,0:T(8,128)(2,1)}, bf16[11,3,128,128]{3,2,1,0:T(8,128)(2,1)}, u32[]{:S(2)}, u32[]{:S(2)}) collective-permute-start(bf16[11,3,128,128]{3,2,1,0:T(8,128)(2,1)} %collective-permute-done.14.k_ref), channel_id=1, source_target_pairs={{0,4},{1,5},{4,8},{5,9},{6,2},{7,3},{8,12},{9,13},{10,6},{11,7},{1... | collective-permute-start | bytes 3244040 | tf_op jit(solution)/shard_map/cond/branch_2_fun/ppermute | solution.py:331
  95.7 1.6 collective-permute-start.20
  97.3 1.0 dynamic-slice_bitcast_fusion.9
  98.3 33.4 %collective-permute-done.18.v_ref = bf16[11,3,128,128]{3,2,1,0:T(8,128)(2,1)} collective-permute-done((bf16[11,3,128,128]{3,2,1,0:T(8,128)(2,1)}, bf16[11,3,128,128]{3,2,1,0:T(8,128)(2,1)}, u32[]{:S(2)}, u32[]{:S(2)}) %collective-permute-start.18) | collective-permute-done | bytes 1081376 | tf_op jit(solution)/shard_map/cond/branch_2_fun/ppermute | solution.py:331
  131.7 1.0 dynamic-slice_bitcast_fusion.8
  132.7 1.0 pad_maximum_fusion.5
  133.7 2.0 collective-permute-start.19
  135.7 0.0 collective-permute-done.16.v_ref
  135.7 0.0 copy-start.7
  135.7 0.8 collective-permute-done.15.k_ref
  136.5 1.0 dynamic-slice_bitcast_fusion.11
  137.5 0.9 pad_maximum_fusion.4
  138.4 1.0 collective-permute-start.17
  139.4 0.0 collective-permute-done.20.edge_ref
  139.4 0.0 copy-done.2
  139.4 0.0 copy-done.14
  139.4 21.3 %local.7 = (f32[3,128,2560]{2,1,0:T(8,128)}, f32[3,128,2560]{2,1,0:T(8,128)}, f32[3,128,2560]{2,1,0:T(8,128)}) custom-call(s32[20]{0:T(128)S(1)} %copy-done.14, s32[1]{0:T(128)} %get-tuple-element.154.device, bf16[3,128,2560]{2,1,0:T(8,128)(2,1)S(1)} %copy-done.2, bf16[3,128,2560]{2,1,0:T(8,128)(2,1)} %get-tuple-element.157.key_hbm.k_ref, ...), custom_call_target="tpu_custom_call" | custom-call | flops 1509949440 | bytes 19660800 | tf_op jit(solution)/shard_map/cond/branch_2_fun/local/pallas_call | solution.py:407
  160.7 0.0 copy-done.7
  160.7 0.0 collective-permute-done.19.edge_ref
  160.7 13.8 %time.14 = (f32[3,128,2560]{2,1,0:T(8,128)}, f32[3,128,2560]{2,1,0:T(8,128)}, f32[3,128,2560]{2,1,0:T(8,128)}) custom-call(s32[8,128]{1,0:T(8,128)} %get-tuple-element.249.plan, s32[20]{0:T(128)S(1)} %copy-done.14, s32[1]{0:T(128)} %get-tuple-element.154.device, s32[1]{0:T(128)} %constant.97.clone.valid, ...), custom_call_target="tpu_custom_call", output_to_operand_aliasing={{0}: (8, {}), {1}: (9, {}), {2}: (10, {})} | custom-call | flops 830472192 | bytes 17301504 | tf_op jit(solution)/shard_map/cond/branch_2_fun/time/pallas_call | solution.py:433
  174.4 0.0 collective-permute-done.17.edge_ref
  174.4 13.8 %time.15 = (f32[3,128,2560]{2,1,0:T(8,128)}, f32[3,128,2560]{2,1,0:T(8,128)}, f32[3,128,2560]{2,1,0:T(8,128)}) custom-call(s32[8,128]{1,0:T(8,128)} %get-tuple-element.249.plan, s32[20]{0:T(128)S(1)} %copy-done.14, s32[1]{0:T(128)} %get-tuple-element.154.device, ...), custom_call_target="tpu_custom_call", output_to_operand_aliasing={{0}: (8, {}), {1}: (9, {}), {2}: (10, {})} | custom-call | flops 830472192 | bytes 17301504 | tf_op jit(solution)/shard_map/cond/branch_2_fun/time/pallas_call | solution.py:433
  188.2 0.0 all-to-all-done.2
  188.7 12.7 %far.1 = bf16[3,128,2560]{2,1,0:T(8,128)(2,1)} custom-call(s32[8,128]{1,0:T(8,128)} %get-tuple-element.230.plan, bf16[3,128,2560]{2,1,0:T(8,128)(2,1)} %q_ref.1, f32[3,128,2560]{2,1,0:T(8,128)} %get-tuple-element.231.acc_ref, f32[3,128,2560]{2,1,0:T(8,128)} %get-tuple-element.232.top_ref, f32[3,128,2560]{2,1,0:T(8,128)} %get-tuple-element.233.sum_ref, ...), custom_call_target="tpu_custom_call" | custom-call | flops 1006632960 | bytes 19660800 | tf_op jit(solution)/shard_map/far/pallas_call | solution.py:473
  (1 shorter events, 0.0 us)
Async XLA Ops:
  10.5 177.7 %all-to-all-start.2 = ((bf16[16,2,4,128,128]{4,3,2,1,0:T(8,128)(2,1)}), bf16[16,2,4,128,128]{4,3,2,1,0:T(8,128)(2,1)}, u32[]{:S(2)}, u32[]{:S(2)}) async-start(bf16[16,2,4,128,128]{4,3,2,1,0:T(8,128)(2,1)} %get-tuple-element.176), calls=%async_computation.2 | async-start | bytes 8388608 | tf_op jit(solution)/shard_map/cond/branch_2_fun/all_to_all | solution.py:403
  17.0 122.4 %copy-start.2 = (bf16[3,128,2560]{2,1,0:T(8,128)(2,1)S(1)}, bf16[3,128,2560]{2,1,0:T(8,128)(2,1)}, u32[]{:S(2)}) copy-start(bf16[3,128,2560]{2,1,0:T(8,128)(2,1)} %get-tuple-element.162.q_ref) | copy-start | bytes 5898244 | tf_op jit(solution)/shard_map/cond
  17.0 122.4 %copy-start.14 = (s32[20]{0:T(128)S(1)}, s32[20]{0:T(128)}, u32[]{:S(2)}) copy-start(s32[20]{0:T(128)} %get-tuple-element.160.reach) | copy-start | bytes 244 | tf_op jit(solution)/shard_map/cond
  17.0 52.6 %collective-permute-start.14 = (bf16[11,3,128,128]{3,2,1,0:T(8,128)(2,1)}, bf16[11,3,128,128]{3,2,1,0:T(8,128)(2,1)}, u32[]{:S(2)}, u32[]{:S(2)}) collective-permute-start(bf16[11,3,128,128]{3,2,1,0:T(8,128)(2,1)} %get-tuple-element.163), channel_id=1, source_target_pairs={{0,2},{1,3},{2,0},{3,1},{4,6},{5,7},{6,4},{7,5},{8,10},{9,11},{10,... | collective-permute-start | bytes 3244040 | tf_op jit(solution)/shard_map/cond/branch_2_fun/ppermute | solution.py:331
  17.4 114.3 %collective-permute-start.18 = (bf16[11,3,128,128]{3,2,1,0:T(8,128)(2,1)}, bf16[11,3,128,128]{3,2,1,0:T(8,128)(2,1)}, u32[]{:S(2)}, u32[]{:S(2)}) collective-permute-start(bf16[11,3,128,128]{3,2,1,0:T(8,128)(2,1)} %get-tuple-element.164), channel_id=1, source_target_pairs={{0,2},{1,3},{2,0},{3,1},{4,6},{5,7},{6,4},{7,5},{8,10},{9,11},{10,... | collective-permute-start | bytes 3244040 | tf_op jit(solution)/shard_map/cond/branch_2_fun/ppermute | solution.py:331
  18.6 117.1 %collective-permute-start.16 = (bf16[11,3,128,128]{3,2,1,0:T(8,128)(2,1)}, bf16[11,3,128,128]{3,2,1,0:T(8,128)(2,1)S(1)}, u32[]{:S(2)}, u32[]{:S(2)}) collective-permute-start(bf16[11,3,128,128]{3,2,1,0:T(8,128)(2,1)} %get-tuple-element.164), channel_id=1, source_target_pairs={{2,4},{3,5},{4,2},{5,3},{6,8},{7,9},{8,6},{9,7},{10,12},{11,13},{1... | collective-permute-start | bytes 3244040 | tf_op jit(solution)/shard_map/cond/branch_2_fun/ppermute | solution.py:331
  69.6 66.9 %collective-permute-start.15 = (bf16[11,3,128,128]{3,2,1,0:T(8,128)(2,1)}, bf16[11,3,128,128]{3,2,1,0:T(8,128)(2,1)}, u32[]{:S(2)}, u32[]{:S(2)}) collective-permute-start(bf16[11,3,128,128]{3,2,1,0:T(8,128)(2,1)} %collective-permute-done.14.k_ref), channel_id=1, source_target_pairs={{0,4},{1,5},{4,8},{5,9},{6,2},{7,3},{8,12},{9,13},{10,6},{11,7},{1... | collective-permute-start | bytes 3244040 | tf_op jit(solution)/shard_map/cond/branch_2_fun/ppermute | solution.py:331
  95.7 43.6 %collective-permute-start.20 = (bf16[2,128,2560]{2,1,0:T(8,128)(2,1)}, bf16[2,128,2560]{2,1,0:T(8,128)(2,1)}, u32[]{:S(2)}, u32[]{:S(2)}) collective-permute-start(bf16[2,128,2560]{2,1,0:T(8,128)(2,1)} %get-tuple-element.166), channel_id=1, source_target_pairs={{0,1},{1,0},{2,3},{3,2},{4,5},{5,4},{6,7},{7,6},{8,9},{9,8},{10,11... | collective-permute-start | bytes 3932168 | tf_op jit(solution)/shard_map/cond/branch_2_fun/ppermute | solution.py:331
  133.7 27.0 %collective-permute-start.19 = (bf16[2,11,128,128]{3,2,1,0:T(8,128)(2,1)}, bf16[2,11,128,128]{3,2,1,0:T(8,128)(2,1)}, u32[]{:S(2)}, u32[]{:S(2)}) collective-permute-start(bf16[2,11,128,128]{3,2,1,0:T(8,128)(2,1)} %pad_maximum_fusion.5), channel_id=1, source_target_pairs={{0,1},{1,0},{2,3},{3,2},{4,5},{5,4},{6,7},{7,6},{8,9},{9,8},{10,11... | collective-permute-start | bytes 2162696 | tf_op jit(solution)/shard_map/cond/branch_2_fun/ppermute | solution.py:331
  135.7 25.0 %copy-start.7 = (bf16[11,3,128,128]{3,2,1,0:T(8,128)(2,1)}, bf16[11,3,128,128]{3,2,1,0:T(8,128)(2,1)S(1)}, u32[]{:S(2)}) copy-start(bf16[11,3,128,128]{3,2,1,0:T(8,128)(2,1)S(1)} %collective-permute-done.16.v_ref) | copy-start | bytes 3244036 | tf_op jit(solution)/shard_map/cond
  138.4 36.0 %collective-permute-start.17 = (bf16[2,11,128,128]{3,2,1,0:T(8,128)(2,1)}, bf16[2,11,128,128]{3,2,1,0:T(8,128)(2,1)}, u32[]{:S(2)}, u32[]{:S(2)}) collective-permute-start(bf16[2,11,128,128]{3,2,1,0:T(8,128)(2,1)} %pad_maximum_fusion.4), channel_id=1, source_target_pairs={{0,1},{1,0},{2,3},{3,2},{4,5},{5,4},{6,7},{7,6},{8,9},{9,8},{10,11... | collective-permute-start | bytes 2162696 | tf_op jit(solution)/shard_map/cond/branch_2_fun/ppermute | solution.py:331

commit v2 on v1

--- a/solution.py
+++ b/solution.py
@@ -14,7 +14,8 @@
 BIG_NEG = -1e30
 BIG_INT = 1 << 20
 
-CAPS = (7, 9, 11, 13)
+CAPS = (6, 8, 10, 12, 14)
+GROUP = 2
 
 
 def relay_fits(mesh):
@@ -92,7 +93,10 @@
         def _():
             plan[3, found] = h
 
-        return found + jnp.where(timed[h] > 0, 1, 0)
+        after = found + jnp.where(timed[h] > 0, 1, 0)
+        plan[6, h] = jnp.maximum(after - 1, 0)
+        plan[7, h] = timed[h]
+        return after
 
     found = lax.fori_loop(0, heads, note, jnp.int32(0))
     plan[4, 0] = found
@@ -168,121 +172,172 @@
     )
 
 
-def with_ones(vals):
-    return jnp.concatenate([vals, jnp.ones_like(vals)], axis=1)
-
-
-def around(u, rows):
-    return [u] if not rows else [u - 1, u, u + 1]
-
-
-def softmax_step(blocks, vals, old, factor):
-    width = vals.shape[1]
-    top = jnp.max(functools.reduce(jnp.maximum, blocks), axis=1, keepdims=True)
-    if old is not None:
-        top = jnp.maximum(old[1], top)
-    else:
-        top = jnp.broadcast_to(top, (blocks[0].shape[0], width))
+def window_blocks(sources, rows, q_ref, at, row_pos):
+    tiles, tile_len = q_ref.shape[:2]
+    neg, zero = jnp.float32(BIG_NEG), jnp.float32(0)
+    if not rows:
+        blocks = []
+        for u in range(tiles):
+            raw = scores_of(q_ref[u, :, at], jnp.concatenate([k(u) for k, _ in sources], axis=0))
+            blocks.append([raw[:, i * tile_len : (i + 1) * tile_len] for i in range(len(sources))])
+        return blocks, [[v(u) for _, v in sources] for u in range(tiles)]
+    query = jnp.concatenate([q_ref[u, :, at] for u in range(tiles)], axis=0)
+    keys = [k(w) for k, _ in sources for w in range(tiles + 1)]
+    vals = [v(w) for _, v in sources for w in range(tiles + 1)]
+    raw = scores_of(query, jnp.concatenate(keys, axis=0))
+    blocks = []
+    for u in range(tiles):
+        line = []
+        for i in range(len(keys)):
+            w = i % (tiles + 1)
+            block = raw[u * tile_len : (u + 1) * tile_len, i * tile_len : (i + 1) * tile_len]
+            if w == tiles:
+                sides = [side for side, end in ((1, 0), (0, tiles - 1)) if u == end]
+                if not sides:
+                    block = None
+                else:
+                    block = block + jnp.where(row_pos == sides[0], zero, neg)
+            elif abs(w - u) > 1:
+                block = None
+            line.append(block)
+        blocks.append(line)
+    return blocks, vals
+
+
+def weights_of(line, old_top, factor):
+    live = [block for block in line if block is not None]
+    top = jnp.max(functools.reduce(jnp.maximum, live), axis=1, keepdims=True)
+    if old_top is not None:
+        top = jnp.maximum(old_top, top)
     shift = top * factor
-    weights = [jnp.exp2(block * factor - shift).astype(jnp.bfloat16) for block in blocks]
-    both = jnp.dot(
-        jnp.concatenate(weights, axis=1), with_ones(vals), preferred_element_type=jnp.float32
-    )
-    mixed, total = both[:, :width], both[:, width:]
-    if old is not None:
-        keep = jnp.exp2(old[1] * factor - shift)
-        mixed = old[0] * keep + mixed
-        total = old[2] * keep + total
-    return mixed, top, total
-
-
-def window_kernel(keys, vals, edge_key, edge_val, q_ref, old, new, rows, row_pos, factor):
+    weights = [None if b is None else jnp.exp2(b * factor - shift) for b in line]
+    total = functools.reduce(jnp.add, [w for w in weights if w is not None])
+    total = jnp.sum(total, axis=1, keepdims=True)
+    blank = jnp.zeros(live[0].shape, jnp.bfloat16)
+    rounded = [blank if w is None else w.astype(jnp.bfloat16) for w in weights]
+    return top, total, jnp.concatenate(rounded, axis=1)
+
+
+def product(weights, vals):
+    return jnp.dot(weights, jnp.concatenate(vals, axis=0), preferred_element_type=jnp.float32)
+
+
+def near_kernel(
+    plan, reach, device, valid, q_ref, k_ref, v_ref, edge_ref, hk_ref, hv_ref, side_ref,
+    acc_ref, top_ref, sum_ref, *, factor
+):
+    head = pl.program_id(0)
     tiles, tile_len, _ = q_ref.shape
-    neg, zero = jnp.float32(BIG_NEG), jnp.float32(0)
-    for u in range(tiles):
-        pieces = []
-        for w in around(u, rows):
-            if 0 <= w < tiles:
-                pieces.append((keys(w), vals(w), None))
-            else:
-                on = row_pos == (1 if w < 0 else 0)
-                pieces.append((edge_key(), edge_val(), jnp.where(on, zero, neg)))
-        raw = scores_of(q_ref[u], jnp.concatenate([p[0] for p in pieces], axis=0))
-        blocks = []
-        for at, (_, _, bias) in enumerate(pieces):
-            block = raw[:, at * tile_len : (at + 1) * tile_len]
-            blocks.append(block if bias is None else block + bias)
-        state = None if old is None else [ref[u] for ref in old]
-        result = softmax_step(
-            blocks, jnp.concatenate([p[1] for p in pieces], axis=0), state, factor
-        )
-        for ref, value in zip(new, result):
-            ref[u] = value
-
-
-def local_kernel(reach, device, q_ref, k_ref, v_ref, edge_ref, *new, factor):
-    head = pl.program_id(0)
     row_pos = device[0] % ROW_BLOCKS
+    lanes = lax.broadcasted_iota(jnp.int32, (tile_len, top_ref.shape[-1]), 1)
+    local = (
+        lambda w: k_ref[w] if w < tiles else edge_ref[0],
+        lambda w: v_ref[w] if w < tiles else edge_ref[1],
+    )
+    timed = (
+        lambda w: hk_ref[0, w] if w < tiles else side_ref[0, 0],
+        lambda w: hv_ref[0, w] if w < tiles else side_ref[1, 0],
+    )
+
+    def run(sources, rows):
+        blocks, vals = window_blocks(sources, rows, q_ref, slice(None), row_pos)
+        parts = [weights_of(line, None, factor) for line in blocks]
+        if rows:
+            mixed = product(jnp.concatenate([p[2] for p in parts], axis=0), vals)
+            mixed = [mixed[u * tile_len : (u + 1) * tile_len] for u in range(tiles)]
+        else:
+            mixed = [product(parts[u][2], vals[u]) for u in range(tiles)]
+        for u in range(tiles):
+            acc_ref[u] = mixed[u]
+            top_ref[u] = jnp.where(lanes == head, parts[u][0], top_ref[u])
+            sum_ref[u] = jnp.where(lanes == head, parts[u][1], sum_ref[u])
+
+    with_time = (plan[7, head] > 0) & (valid[0] > 0)
     for rows in (0, 1):
-
-        @pl.when((reach[head] > 0) == bool(rows))
-        def _():
-            window_kernel(
-                lambda w: k_ref[w],
-                lambda w: v_ref[w],
-                lambda: edge_ref[0],
-                lambda: edge_ref[1],
-                q_ref, None, new, rows, row_pos, factor,
+        for time in (0, 1):
+            pl.when((with_time == bool(time)) & ((reach[head] > 0) == bool(rows)))(
+                functools.partial(run, (local, timed) if time else (local,), rows)
             )
 
 
+def column_of(ref, u, lanes, head):
+    return jnp.sum(jnp.where(lanes == head, ref[u], jnp.float32(0)), axis=1, keepdims=True)
+
+
 def time_kernel(
-    plan, reach, device, valid, q_ref, k_ref, v_ref, edge_ref, *refs, factor
+    plan, reach, device, valid, q_ref, hk_ref, hv_ref, side_ref, acc_ref, top_ref, sum_ref,
+    before_ref, out_ref, *, factor
 ):
-    old, new = refs[:3], refs[3:]
     slot = pl.program_id(0)
     head = plan[3, slot]
+    tiles, tile_len, _ = q_ref.shape
     row_pos = device[0] % ROW_BLOCKS
-    go = (slot < plan[4, 0]) & (valid[0] > 0)
+    lanes = lax.broadcasted_iota(jnp.int32, (tile_len, top_ref.shape[-1]), 1)
+    source = (
+        lambda w: hk_ref[0, w] if w < tiles else side_ref[0, 0],
+        lambda w: hv_ref[0, w] if w < tiles else side_ref[1, 0],
+    )
+
+    def run(rows):
+        blocks, vals = window_blocks((source,), rows, q_ref, slice(None), row_pos)
+        tops = [column_of(top_ref, u, lanes, head) for u in range(tiles)]
+        parts = [weights_of(blocks[u], tops[u], factor) for u in range(tiles)]
+        if rows:
+            mixed = product(jnp.concatenate([p[2] for p in parts], axis=0), vals)
+            mixed = [mixed[u * tile_len : (u + 1) * tile_len] for u in range(tiles)]
+        else:
+            mixed = [product(parts[u][2], vals[u]) for u in range(tiles)]
+        for u in range(tiles):
+            top, total, _ = parts[u]
+            keep = jnp.exp2(tops[u] * factor - top * factor)
+            total = keep * column_of(sum_ref, u, lanes, head) + total
+            out_ref[u] = ((acc_ref[u] * keep + mixed[u]) / total).astype(out_ref.dtype)
+
+    count = plan[4, 0]
+    go = (slot < count) & (valid[0] > 0)
     for rows in (0, 1):
-
-        @pl.when(go & ((reach[head] > 0) == bool(rows)))
-        def _():
-            window_kernel(
-                lambda w: k_ref[0, w],
-                lambda w: v_ref[0, w],
-                lambda: edge_ref[0, 0],
-                lambda: edge_ref[1, 0],
-                q_ref, old, new, rows, row_pos, factor,
-            )
-
-    @pl.when((slot < plan[4, 0]) & (valid[0] == 0) | (slot == 0) & (plan[4, 0] == 0))
+        pl.when(go & ((reach[head] > 0) == bool(rows)))(functools.partial(run, rows))
+
+    @pl.when(jnp.logical_not(go) & ((slot < count) | (slot == 0)))
     def _():
-        for before, after in zip(old, new):
-            after[...] = before[...]
+        out_ref[...] = before_ref[...]
 
 
 def far_kernel(plan, q_ref, acc_ref, top_ref, sum_ref, *refs, factor):
-    fars, out_ref = refs[:-1], refs[-1]
+    fars, (out_ref, acc_out, top_out, sum_out) = refs[:-4], refs[-4:]
     step = pl.program_id(0)
     tiles, tile_len, _ = q_ref.shape
-    width = fars[0].shape[-1]
+    width = out_ref.shape[-1] // len(fars)
     neg, zero = jnp.float32(BIG_NEG), jnp.float32(0)
+    lanes = lax.broadcasted_iota(jnp.int32, (tile_len, top_ref.shape[-1]), 1)
     for g, far_ref in enumerate(fars):
+        head = step * len(fars) + g
         at = slice(g * width, (g + 1) * width)
-        word = plan[2, step * len(fars) + g]
-        keys = far_ref[0, 0].reshape(LIST * tile_len, width)
-        vals = far_ref[0, 1].reshape(LIST * tile_len, width)
+        word = plan[2, head]
+        query = jnp.concatenate([q_ref[u, :, at] for u in range(tiles)], axis=0)
+        raw = scores_of(query, jnp.concatenate([far_ref[0, 0, i] for i in range(LIST)], axis=0))
+        lines = []
         for u in range(tiles):
-            raw = scores_of(q_ref[u, :, at], keys)
-            blocks = []
-            for which in range(LIST):
-                live = (word // (1 << (u * LIST + which))) % 2
-                block = raw[:, which * tile_len : (which + 1) * tile_len]
-                blocks.append(block + jnp.where(live > 0, zero, neg))
-            state = (acc_ref[u, :, at], top_ref[u, :, at], sum_ref[u, :, at])
-            mixed, _, total = softmax_step(blocks, vals, state, factor)
-            out_ref[u, :, at] = (mixed / total).astype(out_ref.dtype)
+            line = []
+            for i in range(LIST):
+                live = (word // (1 << (u * LIST + i))) % 2
+                block = raw[u * tile_len : (u + 1) * tile_len, i * tile_len : (i + 1) * tile_len]
+                line.append(block + jnp.where(live > 0, zero, neg))
+            lines.append(line)
+        tops = [column_of(top_ref, u, lanes, head) for u in range(tiles)]
+        parts = [weights_of(lines[u], tops[u], factor) for u in range(tiles)]
+        mixed = product(
+            jnp.concatenate([p[2] for p in parts], axis=0), [far_ref[0, 1, i] for i in range(LIST)]
+        )
+        for u in range(tiles):
+            top, total, _ = parts[u]
+            keep = jnp.exp2(tops[u] * factor - top * factor)
+            total = keep * column_of(sum_ref, u, lanes, head) + total
+            whole = acc_ref[u, :, at] * keep + mixed[u * tile_len : (u + 1) * tile_len]
+            out_ref[u, :, at] = (whole / total).astype(out_ref.dtype)
+            acc_out[u, :, at] = whole
+            top_out[u] = jnp.where(lanes == head, top, top_out[u])
+            sum_out[u] = jnp.where(lanes == head, total, sum_out[u])
 
 
 def any_spec():
@@ -333,7 +388,6 @@
     def at_head(h, *_):
         return (0, 0, h)
 
-    state_shape = [jax.ShapeDtypeStruct((tiles, tile_len, feat), jnp.float32)] * 3
     tile_spec = pl.BlockSpec((tiles, tile_len, width), at_head)
 
     def near(cap):
@@ -403,89 +457,120 @@
         far = lax.all_to_all(far, "seq", split_axis=0, concat_axis=0, tiled=True)
         edge = permute(edge, pair_route)
 
-        pairs = heads * tiles * 3
+        halves = []
+        for halo in (first, second):
+            sides = jnp.stack(
+                [lax.dynamic_index_in_dim(x, side, 1, keepdims=False) for x in halo]
+            )
+            halves.append((halo[0], halo[1], permute(sides, pair_route)))
+
+        def halo_specs(at):
+            block = (1, tiles, tile_len, width)
+            return [
+                pl.BlockSpec(block, lambda s, plan_ref, *_: (plan_ref[6, at(s)], 0, 0, 0)),
+                pl.BlockSpec(block, lambda s, plan_ref, *_: (plan_ref[6, at(s)], 0, 0, 0)),
+                pl.BlockSpec(
+                    (2, 1, tile_len, width), lambda s, plan_ref, *_: (0, plan_ref[6, at(s)], 0, 0)
+                ),
+            ]
+
+        stat_spec = pl.BlockSpec((tiles, tile_len, 128), lambda h, *_: (0, 0, 0))
+        stat_shape = jax.ShapeDtypeStruct((tiles, tile_len, 128), jnp.float32)
+        pairs = (heads + cap) * tiles * 2
         state = pl.pallas_call(
-            functools.partial(local_kernel, factor=factor),
+            functools.partial(near_kernel, factor=factor),
             grid_spec=pltpu.PrefetchScalarGridSpec(
-                num_scalar_prefetch=2,
+                num_scalar_prefetch=4,
                 grid=(heads,),
-                in_specs=[tile_spec] * 3 + [pl.BlockSpec((2, tile_len, width), at_head)],
-                out_specs=[tile_spec] * 3,
-            ),
-            out_shape=state_shape,
+                in_specs=[tile_spec] * 3
+                + [pl.BlockSpec((2, tile_len, width), at_head)]
+                + halo_specs(lambda s: s),
+                out_specs=[tile_spec, stat_spec, stat_spec],
+            ),
+            out_shape=(
+                jax.ShapeDtypeStruct((tiles, tile_len, feat), jnp.float32),
+                stat_shape,
+                stat_shape,
+            ),
             cost_estimate=pl.CostEstimate(
                 flops=pairs * 4 * tile_len * tile_len * width,
                 transcendentals=pairs * tile_len * tile_len,
-                bytes_accessed=10 * tiles * tile_len * feat * 2,
-            ),
-            name="local",
-        )(window_rows, device, queries, keys, values, edge)
+                bytes_accessed=8 * tiles * tile_len * feat * 2,
+            ),
+            name="near",
+        )(plan, window_rows, device, oks[0], queries, keys, values, edge, *halves[0])
+
+        group = GROUP if heads % GROUP == 0 else 1
+        wide_spec = pl.BlockSpec((tiles, tile_len, width * group), at_head)
+
+        def far_spec(g):
+            return pl.BlockSpec(
+                (1, 2, LIST, tile_len, width),
+                lambda s, p: (p[0, s * group + g], 0, p[1, s * group + g], 0, 0),
+            )
+
+        acc_shape = jax.ShapeDtypeStruct((tiles, tile_len, feat), jnp.float32)
+        pairs = heads * tiles * LIST
+        out, *state = pl.pallas_call(
+            functools.partial(far_kernel, factor=factor),
+            grid_spec=pltpu.PrefetchScalarGridSpec(
+                num_scalar_prefetch=1,
+                grid=(heads // group,),
+                in_specs=[wide_spec] * 2
+                + [stat_spec] * 2
+                + [far_spec(g) for g in range(group)],
+                out_specs=[wide_spec] * 2 + [stat_spec] * 2,
+            ),
+            out_shape=(
+                jax.ShapeDtypeStruct(queries.shape, queries.dtype),
+                acc_shape,
+                stat_shape,
+                stat_shape,
+            ),
+            cost_estimate=pl.CostEstimate(
+                flops=pairs * 4 * tile_len * tile_len * width,
+                transcendentals=pairs * tile_len * tile_len,
+                bytes_accessed=8 * tiles * tile_len * feat * 2,
+            ),
+            name="far",
+        )(plan, queries, *state, *([far] * group))
 
         def at_plan(s, plan_ref, *_):
             return (0, 0, plan_ref[3, s])
 
         planned = pl.BlockSpec((tiles, tile_len, width), at_plan)
+        halo_spec = pl.BlockSpec((1, tiles, tile_len, width), lambda s, *_: (s, 0, 0, 0))
         pairs = cap * tiles * 3
-        for halo, ok in zip((first, second), oks):
-            sides = jnp.stack([lax.dynamic_index_in_dim(x, side, 1, keepdims=False) for x in halo])
-            sides = permute(sides, pair_route)
-            halo_spec = pl.BlockSpec((1, tiles, tile_len, width), lambda s, *_: (s, 0, 0, 0))
-            state = pl.pallas_call(
-                functools.partial(time_kernel, factor=factor),
-                grid_spec=pltpu.PrefetchScalarGridSpec(
-                    num_scalar_prefetch=4,
-                    grid=(cap,),
-                    in_specs=[
-                        planned,
-                        halo_spec,
-                        halo_spec,
-                        pl.BlockSpec((2, 1, tile_len, width), lambda s, *_: (0, s, 0, 0)),
-                        planned,
-                        planned,
-                        planned,
-                    ],
-                    out_specs=[planned] * 3,
-                ),
-                out_shape=state_shape,
-                input_output_aliases={8: 0, 9: 1, 10: 2},
-                cost_estimate=pl.CostEstimate(
-                    flops=pairs * 4 * tile_len * tile_len * width,
-                    transcendentals=pairs * tile_len * tile_len,
-                    bytes_accessed=16 * cap * tiles * pair_tile,
-                ),
-                name="time",
-            )(plan, window_rows, device, ok, queries, halo[0], halo[1], sides, *state)
-        return (*state, far, plan)
+        return pl.pallas_call(
+            functools.partial(time_kernel, factor=factor),
+            grid_spec=pltpu.PrefetchScalarGridSpec(
+                num_scalar_prefetch=4,
+                grid=(cap,),
+                in_specs=[
+                    planned,
+                    halo_spec,
+                    halo_spec,
+                    pl.BlockSpec((2, 1, tile_len, width), lambda s, *_: (0, s, 0, 0)),
+                    planned,
+                    stat_spec,
+                    stat_spec,
+                    planned,
+                ],
+                out_specs=planned,
+            ),
+            out_shape=jax.ShapeDtypeStruct(queries.shape, queries.dtype),
+            input_output_aliases={11: 0},
+            cost_estimate=pl.CostEstimate(
+                flops=pairs * 4 * tile_len * tile_len * width,
+                transcendentals=pairs * tile_len * tile_len,
+                bytes_accessed=8 * cap * tiles * pair_tile,
+            ),
+            name="time",
+        )(plan, window_rows, device, oks[1], queries, *halves[1], *state, out)
 
     caps = [c for c in CAPS if c < heads] + [heads]
     pick = sum((timed_count > c).astype(jnp.int32) for c in caps[:-1])
-    *state, far, plan = lax.switch(pick, [functools.partial(near, c) for c in caps])
-
-    group = 2 if heads % 2 == 0 else 1
-    wide_spec = pl.BlockSpec((tiles, tile_len, width * group), at_head)
-
-    def far_spec(g):
-        return pl.BlockSpec(
-            (1, 2, LIST, tile_len, width),
-            lambda h, plan_ref: (plan_ref[0, h * group + g], 0, plan_ref[1, h * group + g], 0, 0),
-        )
-
-    return pl.pallas_call(
-        functools.partial(far_kernel, factor=factor),
-        grid_spec=pltpu.PrefetchScalarGridSpec(
-            num_scalar_prefetch=1,
-            grid=(heads // group,),
-            in_specs=[wide_spec] * 4 + [far_spec(g) for g in range(group)],
-            out_specs=wide_spec,
-        ),
-        out_shape=jax.ShapeDtypeStruct(queries.shape, queries.dtype),
-        cost_estimate=pl.CostEstimate(
-            flops=heads * tiles * LIST * 4 * tile_len * tile_len * width,
-            transcendentals=heads * tiles * LIST * tile_len * tile_len,
-            bytes_accessed=10 * tiles * tile_len * feat * 2,
-        ),
-        name="far",
-    )(plan, queries, *state, *([far] * group))
+    return lax.switch(pick, [functools.partial(near, c) for c in caps])
 
 
 def solution(mesh):

time: 203 us -> 184 us (0.906)
  Pallas kernels: 68.1 us -> 51.1 us
    pallas_call x2 -> x1, Pallas kernels: 27.5 us -> 10.5 us  [near_of(): pl.pallas_call(functools.partial(time_kernel, factor=factor), grid_spec=p...]
  transfers between devices with their start and end apart: 8 -> 8, of which waited for: 3 -> 4; matrix products, arithmetic and copies ran while one was open for 2% -> 2% of each run, Pallas kernels for 24% -> 19%
where the time goes in v2:
time: 184 us; the launch traced here: 183 us
  waiting for transfers between devices  81.6 us (44%)
  Pallas kernels  51.1 us (28%)
  starting transfers between devices  40.6 us (22%)
  between operations  3.42 us (2%)
  other arithmetic  3.08 us (2%)
  local copies, waits for them, and re-layouts  3 us (2%)
    ppermute x7, waiting for transfers between devices, permute(): return lax.ppermute(value, 'seq', route)  81.6 us
    ppermute x7, starting transfers between devices, permute(): return lax.ppermute(value, 'seq', route)  33.9 us
    pallas_call x1, Pallas kernels, near_of(): pl.pallas_call(functools.partial(near_kernel, factor=factor), grid_spec=p...  22 us
    pallas_call x1, Pallas kernels, near_of(): pl.pallas_call(functools.partial(far_kernel, factor=factor), grid_spec=pl...  12.1 us
    pallas_call x1, Pallas kernels, near_of(): pl.pallas_call(functools.partial(time_kernel, factor=factor), grid_spec=p...  10.5 us
    all_to_all x1, starting transfers between devices, near_of(): far = lax.all_to_all(far, 'seq', split_axis=0, concat_axis=0, tiled=True)  6.67 us
    pallas_call x1, Pallas kernels, near_of(): pl.pallas_call(pack_kernel, out_shape=(halo_shape, halo_shape, jax.ShapeD...  6.52 us
  transfers between devices with their start and end apart: 8, of which 4 were waited for; matrix products, arithmetic and copies ran while one was open for 2% of the time, Pallas kernels for 19%

profile of v2, /device:TPU:13, one launch (start us, length us, event | category | flops | bytes accessed | tf_op | source)
XLA Modules:
  0.0 182.9 jit_solution(4174144307506218223)
XLA Ops:
  0.0 1.3 fusion
  4.5 178.2 %conditional.1 = (bf16[3,128,2560]{2,1,0:T(8,128)(2,1)}) conditional(s32[]{:T(128)} %clamp.3, (s32[20]{0:T(128)}, s32[]{:T(128)}, s32[20,2,48]{2,1,0:T(2,128)}, s32[20,48]{1,0:T(8,128)}, bf16[3,128,2560]{2,1,0:T(8,128)(2,1)}, /*index=5*/bf16[3,128,2560]{2,1,0:T(8,128)(2,1)}, s32[]{:T(128)}, s32[20]{0:T(128)}, ...), branch_computations={%region_1.2_spmd, %region_2.3_spmd, %region_3.4_spmd, %region_4.5_... | conditional | flops 4531159040 | bytes 146539424 | solution.py:573
  4.6 6.5 %pack.8 = (bf16[10,3,128,128]{3,2,1,0:T(8,128)(2,1)}, bf16[10,3,128,128]{3,2,1,0:T(8,128)(2,1)}, bf16[2,128,2560]{2,1,0:T(8,128)(2,1)}, bf16[16,2,4,128,128]{4,3,2,1,0:T(8,128)(2,1)}, s32[8,128]{1,0:T(8,128)}) custom-call(s32[20]{0:T(128)} %get-tuple-element.176.timed, s32[1]{0:T(128)} %bitcast.12.device, s32[20,2,48]{2,1,0:T(2,128)} %get-tuple-element.178.lists.lists_s, ...), custom_call_target="tpu_custom_call" | custom-call | bytes 6160384 | tf_op jit(solution)/shard_map/cond/branch_2_fun/pack/pallas_call | solution.py:398
  11.1 0.0 copy-start.23
  11.1 6.7 %all-to-all-start.2 = ((bf16[16,2,4,128,128]{4,3,2,1,0:T(8,128)(2,1)}), bf16[16,2,4,128,128]{4,3,2,1,0:T(8,128)(2,1)}, u32[]{:S(2)}, u32[]{:S(2)}) async-start(bf16[16,2,4,128,128]{4,3,2,1,0:T(8,128)(2,1)} %get-tuple-element.193), calls=%async_computation.2 | async-start | bytes 8388608 | tf_op jit(solution)/shard_map/cond/branch_2_fun/all_to_all | solution.py:457
  17.8 0.0 copy-done.23
  17.8 0.3 collective-permute-start.14
  18.1 1.2 collective-permute-start.19
  19.3 3.1 %collective-permute-start.16 = (bf16[10,3,128,128]{3,2,1,0:T(8,128)(2,1)}, bf16[10,3,128,128]{3,2,1,0:T(8,128)(2,1)S(1)}, u32[]{:S(2)}, u32[]{:S(2)}) collective-permute-start(bf16[10,3,128,128]{3,2,1,0:T(8,128)(2,1)} %get-tuple-element.187), channel_id=1, source_target_pairs={{2,4},{3,5},{4,2},{5,3},{6,8},{7,9},{8,6},{9,7},{10,12},{11,13},{1... | collective-permute-start | bytes 2949128 | tf_op jit(solution)/shard_map/cond/branch_2_fun/ppermute | solution.py:386
  22.4 45.8 %collective-permute-done.14.hk_ref = bf16[10,3,128,128]{3,2,1,0:T(8,128)(2,1)} collective-permute-done((bf16[10,3,128,128]{3,2,1,0:T(8,128)(2,1)S(1)}, bf16[10,3,128,128]{3,2,1,0:T(8,128)(2,1)}, u32[]{:S(2)}, u32[]{:S(2)}) %collective-permute-start.14) | collective-permute-done | bytes 983072 | tf_op jit(solution)/shard_map/cond/branch_2_fun/ppermute | solution.py:386
  68.2 26.1 %collective-permute-start.15 = (bf16[10,3,128,128]{3,2,1,0:T(8,128)(2,1)}, bf16[10,3,128,128]{3,2,1,0:T(8,128)(2,1)}, u32[]{:S(2)}, u32[]{:S(2)}) collective-permute-start(bf16[10,3,128,128]{3,2,1,0:T(8,128)(2,1)} %collective-permute-done.14.hk_ref), channel_id=1, source_target_pairs={{0,4},{1,5},{4,8},{5,9},{6,2},{7,3},{8,12},{9,13},{10,6},{11,7},{1... | collective-permute-start | bytes 2949128 | tf_op jit(solution)/shard_map/cond/branch_2_fun/ppermute | solution.py:386
  94.3 1.2 collective-permute-start.18
  95.6 1.0 dynamic-slice_bitcast_fusion.9
  96.6 29.6 %collective-permute-done.19.hv_ref = bf16[10,3,128,128]{3,2,1,0:T(8,128)(2,1)S(1)} collective-permute-done((bf16[10,3,128,128]{3,2,1,0:T(8,128)(2,1)}, bf16[10,3,128,128]{3,2,1,0:T(8,128)(2,1)S(1)}, u32[]{:S(2)}, u32[]{:S(2)}) %collective-permute-start.19) | collective-permute-done | bytes 983072 | tf_op jit(solution)/shard_map/cond/branch_2_fun/ppermute | solution.py:386
  126.2 0.0 copy-start.12
  126.2 0.9 copy-done.12
  127.1 0.0 copy-start.2
  127.1 0.0 copy-start.19
  127.2 0.9 pad_maximum_fusion.5
  128.1 1.0 collective-permute-start.20
  129.0 2.1 %collective-permute-done.16.hv_ref = bf16[10,3,128,128]{3,2,1,0:T(8,128)(2,1)S(1)} collective-permute-done((bf16[10,3,128,128]{3,2,1,0:T(8,128)(2,1)}, bf16[10,3,128,128]{3,2,1,0:T(8,128)(2,1)S(1)}, u32[]{:S(2)}, u32[]{:S(2)}) %collective-permute-start.16) | collective-permute-done | bytes 983072 | tf_op jit(solution)/shard_map/cond/branch_2_fun/ppermute | solution.py:386
  131.1 0.0 copy-start.11
  131.1 4.1 %collective-permute-done.15.hk_ref = bf16[10,3,128,128]{3,2,1,0:T(8,128)(2,1)} collective-permute-done((bf16[10,3,128,128]{3,2,1,0:T(8,128)(2,1)}, bf16[10,3,128,128]{3,2,1,0:T(8,128)(2,1)}, u32[]{:S(2)}, u32[]{:S(2)}) %collective-permute-start.15) | collective-permute-done | bytes 983072 | tf_op jit(solution)/shard_map/cond/branch_2_fun/ppermute | solution.py:386
  135.2 1.0 dynamic-slice_bitcast_fusion.11
  136.2 0.9 pad_maximum_fusion.4
  137.1 1.0 collective-permute-start.17
  138.1 0.0 collective-permute-done.18.edge_ref
  138.1 0.0 collective-permute-done.20.side_ref
  138.1 0.0 copy-done.2
  138.1 0.0 copy-done.19
  138.1 22.0 %near.8 = (f32[3,128,2560]{2,1,0:T(8,128)}, f32[3,128,128]{2,1,0:T(8,128)}, f32[3,128,128]{2,1,0:T(8,128)}) custom-call(s32[8,128]{1,0:T(8,128)} %get-tuple-element.182.plan, s32[20]{0:T(128)S(1)} %copy-done.19, s32[1]{0:T(128)} %bitcast.12.device, s32[1]{0:T(128)} %constant.110.clone.valid, bf16[3,128,2560]{2,1,0:T(8,128)(2,1)S(1)} %copy-done.2, ...), custom_call_target="tpu_custom_call" | custom-call | flops 1509949440 | bytes 15728640 | tf_op jit(solution)/shard_map/cond/branch_2_fun/near/pallas_call | solution.py:480
  160.1 0.0 copy-done.11
  160.1 0.0 all-to-all-done.2.refs_0_.refs_1_
  160.1 12.1 %far.8 = (bf16[3,128,2560]{2,1,0:T(8,128)(2,1)}, f32[3,128,2560]{2,1,0:T(8,128)}, f32[3,128,128]{2,1,0:T(8,128)}, f32[3,128,128]{2,1,0:T(8,128)}) custom-call(s32[8,128]{1,0:T(8,128)} %get-tuple-element.182.plan, bf16[3,128,2560]{2,1,0:T(8,128)(2,1)S(1)} %copy-done.2, f32[3,128,2560]{2,1,0:T(8,128)} %get-tuple-element.190.acc_ref, ...), custom_call_target="tpu_custom_call" | custom-call | flops 1006632960 | bytes 15728640 | tf_op jit(solution)/shard_map/cond/branch_2_fun/far/pallas_call | solution.py:514
  172.2 0.0 collective-permute-done.17.side_ref
  172.2 10.5 %time.8 = bf16[3,128,2560]{2,1,0:T(8,128)(2,1)} custom-call(s32[8,128]{1,0:T(8,128)} %get-tuple-element.182.plan, s32[20]{0:T(128)S(1)} %copy-done.19, s32[1]{0:T(128)} %bitcast.12.device, s32[1]{0:T(128)} %bitcast.13.valid, bf16[3,128,2560]{2,1,0:T(8,128)(2,1)S(1)} %copy-done.2, ...), custom_call_target="tpu_custom_call", output_to_operand_aliasing={{}: (11, {})} | custom-call | flops 754974720 | bytes 7864320 | tf_op jit(solution)/shard_map/cond/branch_2_fun/time/pallas_call | solution.py:544
  (2 shorter events, 0.0 us)
Async XLA Ops:
  11.1 6.7 %copy-start.23 = (bf16[10,3,128,128]{3,2,1,0:T(8,128)(2,1)S(1)}, bf16[10,3,128,128]{3,2,1,0:T(8,128)(2,1)}, u32[]{:S(2)}) copy-start(bf16[10,3,128,128]{3,2,1,0:T(8,128)(2,1)} %get-tuple-element.186) | copy-start | bytes 2949124 | tf_op jit(solution)/shard_map/cond
  11.1 148.9 %all-to-all-start.2 = ((bf16[16,2,4,128,128]{4,3,2,1,0:T(8,128)(2,1)}), bf16[16,2,4,128,128]{4,3,2,1,0:T(8,128)(2,1)}, u32[]{:S(2)}, u32[]{:S(2)}) async-start(bf16[16,2,4,128,128]{4,3,2,1,0:T(8,128)(2,1)} %get-tuple-element.193), calls=%async_computation.2 | async-start | bytes 8388608 | tf_op jit(solution)/shard_map/cond/branch_2_fun/all_to_all | solution.py:457
  17.8 50.4 %collective-permute-start.14 = (bf16[10,3,128,128]{3,2,1,0:T(8,128)(2,1)S(1)}, bf16[10,3,128,128]{3,2,1,0:T(8,128)(2,1)}, u32[]{:S(2)}, u32[]{:S(2)}) collective-permute-start(bf16[10,3,128,128]{3,2,1,0:T(8,128)(2,1)S(1)} %copy-done.23), channel_id=1, source_target_pairs={{0,2},{1,3},{2,0},{3,1},{4,6},{5,7},{6,4},{7,5},{8,10},{9,11},{10,... | collective-permute-start | bytes 2949128 | tf_op jit(solution)/shard_map/cond/branch_2_fun/ppermute | solution.py:386
  18.1 108.0 %collective-permute-start.19 = (bf16[10,3,128,128]{3,2,1,0:T(8,128)(2,1)}, bf16[10,3,128,128]{3,2,1,0:T(8,128)(2,1)S(1)}, u32[]{:S(2)}, u32[]{:S(2)}) collective-permute-start(bf16[10,3,128,128]{3,2,1,0:T(8,128)(2,1)} %get-tuple-element.187), channel_id=1, source_target_pairs={{0,2},{1,3},{2,0},{3,1},{4,6},{5,7},{6,4},{7,5},{8,10},{9,11},{10,... | collective-permute-start | bytes 2949128 | tf_op jit(solution)/shard_map/cond/branch_2_fun/ppermute | solution.py:386
  19.3 111.8 %collective-permute-start.16 = (bf16[10,3,128,128]{3,2,1,0:T(8,128)(2,1)}, bf16[10,3,128,128]{3,2,1,0:T(8,128)(2,1)S(1)}, u32[]{:S(2)}, u32[]{:S(2)}) collective-permute-start(bf16[10,3,128,128]{3,2,1,0:T(8,128)(2,1)} %get-tuple-element.187), channel_id=1, source_target_pairs={{2,4},{3,5},{4,2},{5,3},{6,8},{7,9},{8,6},{9,7},{10,12},{11,13},{1... | collective-permute-start | bytes 2949128 | tf_op jit(solution)/shard_map/cond/branch_2_fun/ppermute | solution.py:386
  68.2 67.0 %collective-permute-start.15 = (bf16[10,3,128,128]{3,2,1,0:T(8,128)(2,1)}, bf16[10,3,128,128]{3,2,1,0:T(8,128)(2,1)}, u32[]{:S(2)}, u32[]{:S(2)}) collective-permute-start(bf16[10,3,128,128]{3,2,1,0:T(8,128)(2,1)} %collective-permute-done.14.hk_ref), channel_id=1, source_target_pairs={{0,4},{1,5},{4,8},{5,9},{6,2},{7,3},{8,12},{9,13},{10,6},{11,7},{1... | collective-permute-start | bytes 2949128 | tf_op jit(solution)/shard_map/cond/branch_2_fun/ppermute | solution.py:386
  94.3 43.7 %collective-permute-start.18 = (bf16[2,128,2560]{2,1,0:T(8,128)(2,1)}, bf16[2,128,2560]{2,1,0:T(8,128)(2,1)}, u32[]{:S(2)}, u32[]{:S(2)}) collective-permute-start(bf16[2,128,2560]{2,1,0:T(8,128)(2,1)} %get-tuple-element.189), channel_id=1, source_target_pairs={{0,1},{1,0},{2,3},{3,2},{4,5},{5,4},{6,7},{7,6},{8,9},{9,8},{10,11... | collective-permute-start | bytes 3932168 | tf_op jit(solution)/shard_map/cond/branch_2_fun/ppermute | solution.py:386
  126.2 0.9 copy-start.12
  127.1 11.0 %copy-start.2 = (bf16[3,128,2560]{2,1,0:T(8,128)(2,1)S(1)}, bf16[3,128,2560]{2,1,0:T(8,128)(2,1)}, u32[]{:S(2)}) copy-start(bf16[3,128,2560]{2,1,0:T(8,128)(2,1)} %get-tuple-element.351.q_ref) | copy-start | bytes 5898244 | tf_op jit(solution)/shard_map/cond
  127.1 10.9 %copy-start.19 = (s32[20]{0:T(128)S(1)}, s32[20]{0:T(128)}, u32[]{:S(2)}) copy-start(s32[20]{0:T(128)} %get-tuple-element.345.reach) | copy-start | bytes 244 | tf_op jit(solution)/shard_map/cond
  128.1 10.0 %collective-permute-start.20 = (bf16[2,10,128,128]{3,2,1,0:T(8,128)(2,1)}, bf16[2,10,128,128]{3,2,1,0:T(8,128)(2,1)}, u32[]{:S(2)}, u32[]{:S(2)}) collective-permute-start(bf16[2,10,128,128]{3,2,1,0:T(8,128)(2,1)} %pad_maximum_fusion.5), channel_id=1, source_target_pairs={{0,1},{1,0},{2,3},{3,2},{4,5},{5,4},{6,7},{7,6},{8,9},{9,8},{10,11... | collective-permute-start | bytes 1966088 | tf_op jit(solution)/shard_map/cond/branch_2_fun/ppermute | solution.py:386
  131.1 29.0 %copy-start.11 = (bf16[10,3,128,128]{3,2,1,0:T(8,128)(2,1)}, bf16[10,3,128,128]{3,2,1,0:T(8,128)(2,1)S(1)}, u32[]{:S(2)}) copy-start(bf16[10,3,128,128]{3,2,1,0:T(8,128)(2,1)S(1)} %collective-permute-done.16.hv_ref) | copy-start | bytes 2949124 | tf_op jit(solution)/shard_map/cond
  137.1 35.1 %collective-permute-start.17 = (bf16[2,10,128,128]{3,2,1,0:T(8,128)(2,1)}, bf16[2,10,128,128]{3,2,1,0:T(8,128)(2,1)}, u32[]{:S(2)}, u32[]{:S(2)}) collective-permute-start(bf16[2,10,128,128]{3,2,1,0:T(8,128)(2,1)} %pad_maximum_fusion.4), channel_id=1, source_target_pairs={{0,1},{1,0},{2,3},{3,2},{4,5},{5,4},{6,7},{7,6},{8,9},{9,8},{10,11... | collective-permute-start | bytes 1966088 | tf_op jit(solution)/shard_map/cond/branch_2_fun/ppermute | solution.py:386

commit v3 on v2

--- a/solution.py
+++ b/solution.py
@@ -14,7 +14,7 @@
 BIG_NEG = -1e30
 BIG_INT = 1 << 20
 
-CAPS = (6, 8, 10, 12, 14)
+CAPS = (8, 10, 12, 14, 17)
 GROUP = 2
 
 
@@ -223,7 +223,7 @@
 
 
 def near_kernel(
-    plan, reach, device, valid, q_ref, k_ref, v_ref, edge_ref, hk_ref, hv_ref, side_ref,
+    plan, reach, device, valid, q_ref, k_ref, v_ref, edge_ref, hk_ref, hv_ref, sk_ref, sv_ref,
     acc_ref, top_ref, sum_ref, *, factor
 ):
     head = pl.program_id(0)
@@ -235,8 +235,8 @@
         lambda w: v_ref[w] if w < tiles else edge_ref[1],
     )
     timed = (
-        lambda w: hk_ref[0, w] if w < tiles else side_ref[0, 0],
-        lambda w: hv_ref[0, w] if w < tiles else side_ref[1, 0],
+        lambda w: hk_ref[0, w] if w < tiles else sk_ref[0],
+        lambda w: hv_ref[0, w] if w < tiles else sv_ref[0],
     )
 
     def run(sources, rows):
@@ -265,8 +265,8 @@
 
 
 def time_kernel(
-    plan, reach, device, valid, q_ref, hk_ref, hv_ref, side_ref, acc_ref, top_ref, sum_ref,
-    before_ref, out_ref, *, factor
+    plan, reach, device, valid, q_ref, hk_ref, hv_ref, sk_ref, sv_ref, acc_ref, top_ref, sum_ref,
+    _, out_ref, *, factor
 ):
     slot = pl.program_id(0)
     head = plan[3, slot]
@@ -274,8 +274,8 @@
     row_pos = device[0] % ROW_BLOCKS
     lanes = lax.broadcasted_iota(jnp.int32, (tile_len, top_ref.shape[-1]), 1)
     source = (
-        lambda w: hk_ref[0, w] if w < tiles else side_ref[0, 0],
-        lambda w: hv_ref[0, w] if w < tiles else side_ref[1, 0],
+        lambda w: hk_ref[0, w] if w < tiles else sk_ref[0],
+        lambda w: hv_ref[0, w] if w < tiles else sv_ref[0],
     )
 
     def run(rows):
@@ -300,7 +300,8 @@
 
     @pl.when(jnp.logical_not(go) & ((slot < count) | (slot == 0)))
     def _():
-        out_ref[...] = before_ref[...]
+        for u in range(tiles):
+            out_ref[u] = (acc_ref[u] / column_of(sum_ref, u, lanes, head)).astype(out_ref.dtype)
 
 
 def far_kernel(plan, q_ref, acc_ref, top_ref, sum_ref, *refs, factor):
@@ -457,22 +458,21 @@
         far = lax.all_to_all(far, "seq", split_axis=0, concat_axis=0, tiled=True)
         edge = permute(edge, pair_route)
 
-        halves = []
-        for halo in (first, second):
-            sides = jnp.stack(
-                [lax.dynamic_index_in_dim(x, side, 1, keepdims=False) for x in halo]
-            )
-            halves.append((halo[0], halo[1], permute(sides, pair_route)))
+        def side_of(value):
+            return permute(lax.dynamic_index_in_dim(value, side, 1, keepdims=False), pair_route)
+
+        halves = [(*halo, *[side_of(x) for x in halo]) for halo in (first, second)]
 
         def halo_specs(at):
-            block = (1, tiles, tile_len, width)
-            return [
-                pl.BlockSpec(block, lambda s, plan_ref, *_: (plan_ref[6, at(s)], 0, 0, 0)),
-                pl.BlockSpec(block, lambda s, plan_ref, *_: (plan_ref[6, at(s)], 0, 0, 0)),
-                pl.BlockSpec(
-                    (2, 1, tile_len, width), lambda s, plan_ref, *_: (0, plan_ref[6, at(s)], 0, 0)
-                ),
-            ]
+            def whole(s, plan_ref, *_):
+                return (plan_ref[6, at(s)], 0, 0, 0)
+
+            def part(s, plan_ref, *_):
+                return (plan_ref[6, at(s)], 0, 0)
+
+            return [pl.BlockSpec((1, tiles, tile_len, width), whole)] * 2 + [
+                pl.BlockSpec((1, tile_len, width), part)
+            ] * 2
 
         stat_spec = pl.BlockSpec((tiles, tile_len, 128), lambda h, *_: (0, 0, 0))
         stat_shape = jax.ShapeDtypeStruct((tiles, tile_len, 128), jnp.float32)
@@ -540,6 +540,7 @@
 
         planned = pl.BlockSpec((tiles, tile_len, width), at_plan)
         halo_spec = pl.BlockSpec((1, tiles, tile_len, width), lambda s, *_: (s, 0, 0, 0))
+        side_spec = pl.BlockSpec((1, tile_len, width), lambda s, *_: (s, 0, 0))
         pairs = cap * tiles * 3
         return pl.pallas_call(
             functools.partial(time_kernel, factor=factor),
@@ -550,16 +551,17 @@
                     planned,
                     halo_spec,
                     halo_spec,
-                    pl.BlockSpec((2, 1, tile_len, width), lambda s, *_: (0, s, 0, 0)),
+                    side_spec,
+                    side_spec,
                     planned,
                     stat_spec,
                     stat_spec,
-                    planned,
+                    any_spec(),
                 ],
                 out_specs=planned,
             ),
             out_shape=jax.ShapeDtypeStruct(queries.shape, queries.dtype),
-            input_output_aliases={11: 0},
+            input_output_aliases={12: 0},
             cost_estimate=pl.CostEstimate(
                 flops=pairs * 4 * tile_len * tile_len * width,
                 transcendentals=pairs * tile_len * tile_len,

time: 184 us -> 185 us (level)
  the two profiles are of different devices: /device:TPU:13 before, /device:TPU:15 now
where the time goes in v3:
time: 185 us; the launch traced here: 183 us
  waiting for transfers between devices  78.2 us (42%)
  Pallas kernels  51 us (28%)
  starting transfers between devices  42.4 us (23%)
  local copies, waits for them, and re-layouts  6.72 us (4%)
  between operations  3.42 us (2%)
    ppermute x9, waiting for transfers between devices, permute(): return lax.ppermute(value, 'seq', route)  78.2 us
    ppermute x9, starting transfers between devices, permute(): return lax.ppermute(value, 'seq', route)  35.9 us
    pallas_call x1, Pallas kernels, near_of(): pl.pallas_call(functools.partial(near_kernel, factor=factor), grid_spec=p...  22.1 us
    pallas_call x1, Pallas kernels, near_of(): pl.pallas_call(functools.partial(far_kernel, factor=factor), grid_spec=pl...  12 us
    pallas_call x1, Pallas kernels, near_of(): pl.pallas_call(functools.partial(time_kernel, factor=factor), grid_spec=p...  10.3 us
    all_to_all x1, starting transfers between devices, near_of(): far = lax.all_to_all(far, 'seq', split_axis=0, concat_axis=0, tiled=True)  6.53 us
    pallas_call x1, Pallas kernels, near_of(): pl.pallas_call(pack_kernel, out_shape=(halo_shape, halo_shape, jax.ShapeD...  6.53 us
    squeeze x4, local copies, waits for them, and re-layouts, side_of(): lax.dynamic_index_in_dim(value, side, 1, keepdims=False)  6.01 us
  transfers between devices with their start and end apart: 10, of which 4 were waited for; matrix products, arithmetic and copies ran while one was open for 3% of the time, Pallas kernels for 19%

profile of v3, /device:TPU:15, one launch (start us, length us, event | category | flops | bytes accessed | tf_op | source)
XLA Modules:
  0.0 183.2 jit_solution(4680928944372747987)
XLA Ops:
  0.0 1.3 fusion
  4.5 178.5 %conditional.1 = (bf16[3,128,2560]{2,1,0:T(8,128)(2,1)}) conditional(s32[]{:T(128)} %clamp.3, (s32[20]{0:T(128)}, s32[]{:T(128)}, s32[20,2,48]{2,1,0:T(2,128)}, s32[20,48]{1,0:T(8,128)}, bf16[3,128,2560]{2,1,0:T(8,128)(2,1)}, /*index=5*/bf16[3,128,2560]{2,1,0:T(8,128)(2,1)}, s32[]{:T(128)}, s32[20]{0:T(128)}, ...), branch_computations={%region_1.2_spmd, %region_2.3_spmd, %region_3.4_spmd, %region_4.5_... | conditional | flops 4529848320 | bytes 141296640 | solution.py:575
  4.6 6.5 %pack.7 = (bf16[10,3,128,128]{3,2,1,0:T(8,128)(2,1)}, bf16[10,3,128,128]{3,2,1,0:T(8,128)(2,1)}, bf16[2,128,2560]{2,1,0:T(8,128)(2,1)}, bf16[16,2,4,128,128]{4,3,2,1,0:T(8,128)(2,1)}, s32[8,128]{1,0:T(8,128)}) custom-call(s32[20]{0:T(128)} %get-tuple-element.154.timed, s32[1]{0:T(128)} %bitcast.6.device, s32[20,2,48]{2,1,0:T(2,128)} %get-tuple-element.156.lists.lists_s, ...), custom_call_target="tpu_custom_call" | custom-call | bytes 6160384 | tf_op jit(solution)/shard_map/cond/branch_1_fun/pack/pallas_call | solution.py:399
  11.1 6.5 %all-to-all-start.1 = ((bf16[16,2,4,128,128]{4,3,2,1,0:T(8,128)(2,1)}), bf16[16,2,4,128,128]{4,3,2,1,0:T(8,128)(2,1)}, u32[]{:S(2)}, u32[]{:S(2)}) async-start(bf16[16,2,4,128,128]{4,3,2,1,0:T(8,128)(2,1)} %get-tuple-element.171), calls=%async_computation.1 | async-start | bytes 8388608 | tf_op jit(solution)/shard_map/cond/branch_1_fun/all_to_all | solution.py:458
  17.6 0.0 copy-start.1
  17.6 0.0 copy-start.16
  17.7 0.3 collective-permute-start.9
  18.0 1.2 collective-permute-start.15
  19.2 3.1 %collective-permute-start.11 = (bf16[10,3,128,128]{3,2,1,0:T(8,128)(2,1)}, bf16[10,3,128,128]{3,2,1,0:T(8,128)(2,1)S(1)}, u32[]{:S(2)}, u32[]{:S(2)}) collective-permute-start(bf16[10,3,128,128]{3,2,1,0:T(8,128)(2,1)} %get-tuple-element.165), channel_id=1, source_target_pairs={{2,4},{3,5},{4,2},{5,3},{6,8},{7,9},{8,6},{9,7},{10,12},{11,13},{1... | collective-permute-start | bytes 2949128 | tf_op jit(solution)/shard_map/cond/branch_1_fun/ppermute | solution.py:387
  22.3 1.3 collective-permute-start.14
  23.6 44.6 %collective-permute-done.9.hk_ref = bf16[10,3,128,128]{3,2,1,0:T(8,128)(2,1)} collective-permute-done((bf16[10,3,128,128]{3,2,1,0:T(8,128)(2,1)}, bf16[10,3,128,128]{3,2,1,0:T(8,128)(2,1)}, u32[]{:S(2)}, u32[]{:S(2)}) %collective-permute-start.9) | collective-permute-done | bytes 983072 | tf_op jit(solution)/shard_map/cond/branch_1_fun/ppermute | solution.py:387
  68.1 25.9 %collective-permute-start.10 = (bf16[10,3,128,128]{3,2,1,0:T(8,128)(2,1)}, bf16[10,3,128,128]{3,2,1,0:T(8,128)(2,1)}, u32[]{:S(2)}, u32[]{:S(2)}) collective-permute-start(bf16[10,3,128,128]{3,2,1,0:T(8,128)(2,1)} %collective-permute-done.9.hk_ref), channel_id=1, source_target_pairs={{0,4},{1,5},{4,8},{5,9},{6,2},{7,3},{8,12},{9,13},{10,6},{11,7},{1... | collective-permute-start | bytes 2949128 | tf_op jit(solution)/shard_map/cond/branch_1_fun/ppermute | solution.py:387
  94.0 1.7 dynamic-slice_bitcast_fusion.5
  95.8 1.2 collective-permute-start.16
  96.9 29.1 %collective-permute-done.15.hv_ref = bf16[10,3,128,128]{3,2,1,0:T(8,128)(2,1)} collective-permute-done((bf16[10,3,128,128]{3,2,1,0:T(8,128)(2,1)}, bf16[10,3,128,128]{3,2,1,0:T(8,128)(2,1)}, u32[]{:S(2)}, u32[]{:S(2)}) %collective-permute-start.15) | collective-permute-done | bytes 983072 | tf_op jit(solution)/shard_map/cond/branch_1_fun/ppermute | solution.py:387
  126.0 1.7 dynamic-slice_bitcast_fusion.4
  127.8 1.0 collective-permute-start.17
  128.7 2.2 %collective-permute-done.11.hv_ref = bf16[10,3,128,128]{3,2,1,0:T(8,128)(2,1)S(1)} collective-permute-done((bf16[10,3,128,128]{3,2,1,0:T(8,128)(2,1)}, bf16[10,3,128,128]{3,2,1,0:T(8,128)(2,1)S(1)}, u32[]{:S(2)}, u32[]{:S(2)}) %collective-permute-start.11) | collective-permute-done | bytes 983072 | tf_op jit(solution)/shard_map/cond/branch_1_fun/ppermute | solution.py:387
  131.0 0.0 copy-start.8
  131.0 0.8 dynamic-slice_bitcast_fusion.6
  131.8 1.0 collective-permute-start.13
  132.7 2.3 %collective-permute-done.10.hk_ref = bf16[10,3,128,128]{3,2,1,0:T(8,128)(2,1)} collective-permute-done((bf16[10,3,128,128]{3,2,1,0:T(8,128)(2,1)}, bf16[10,3,128,128]{3,2,1,0:T(8,128)(2,1)}, u32[]{:S(2)}, u32[]{:S(2)}) %collective-permute-start.10) | collective-permute-done | bytes 983072 | tf_op jit(solution)/shard_map/cond/branch_1_fun/ppermute | solution.py:387
  135.1 1.7 dynamic-slice_bitcast_fusion.7
  136.8 1.0 collective-permute-start.12
  137.8 0.0 collective-permute-done.16.sk_ref
  137.8 0.0 collective-permute-done.17.sv_ref
  137.8 0.0 collective-permute-done.14.edge_ref
  137.8 0.0 copy-done.1
  137.8 0.0 copy-done.16
  137.8 22.1 %near.7 = (f32[3,128,2560]{2,1,0:T(8,128)}, f32[3,128,128]{2,1,0:T(8,128)}, f32[3,128,128]{2,1,0:T(8,128)}) custom-call(s32[8,128]{1,0:T(8,128)} %get-tuple-element.160.plan, s32[20]{0:T(128)S(1)} %copy-done.16, s32[1]{0:T(128)} %bitcast.6.device, s32[1]{0:T(128)} %constant.107.clone.valid, bf16[3,128,2560]{2,1,0:T(8,128)(2,1)S(1)} %copy-done.1, ...), custom_call_target="tpu_custom_call" | custom-call | flops 1509949440 | bytes 15728640 | tf_op jit(solution)/shard_map/cond/branch_1_fun/near/pallas_call | solution.py:480
  159.9 0.0 copy-done.8
  159.9 0.0 all-to-all-done.1.refs_0_.refs_1_
  160.0 12.0 %far.7 = (bf16[3,128,2560]{2,1,0:T(8,128)(2,1)}, f32[3,128,2560]{2,1,0:T(8,128)}, f32[3,128,128]{2,1,0:T(8,128)}, f32[3,128,128]{2,1,0:T(8,128)}) custom-call(s32[8,128]{1,0:T(8,128)} %get-tuple-element.160.plan, bf16[3,128,2560]{2,1,0:T(8,128)(2,1)S(1)} %copy-done.1, f32[3,128,2560]{2,1,0:T(8,128)} %get-tuple-element.168.acc_ref, ...), custom_call_target="tpu_custom_call" | custom-call | flops 1006632960 | bytes 15728640 | tf_op jit(solution)/shard_map/cond/branch_1_fun/far/pallas_call | solution.py:514
  172.0 0.0 collective-permute-done.13.sv_ref
  172.0 0.0 copy-start.14
  172.0 0.0 collective-permute-done.12.sk_ref
  172.0 0.7 copy-done.14
  172.7 10.3 %time.7 = bf16[3,128,2560]{2,1,0:T(8,128)(2,1)} custom-call(s32[8,128]{1,0:T(8,128)} %get-tuple-element.160.plan, s32[20]{0:T(128)S(1)} %copy-done.16, s32[1]{0:T(128)} %bitcast.6.device, s32[1]{0:T(128)} %bitcast.7.valid, bf16[3,128,2560]{2,1,0:T(8,128)(2,1)S(1)} %copy-done.1, ...), custom_call_target="tpu_custom_call", output_to_operand_aliasing={{}: (12, {})} | custom-call | flops 754974720 | bytes 7864320 | tf_op jit(solution)/shard_map/cond/branch_1_fun/time/pallas_call | solution.py:545
Async XLA Ops:
  11.1 148.8 %all-to-all-start.1 = ((bf16[16,2,4,128,128]{4,3,2,1,0:T(8,128)(2,1)}), bf16[16,2,4,128,128]{4,3,2,1,0:T(8,128)(2,1)}, u32[]{:S(2)}, u32[]{:S(2)}) async-start(bf16[16,2,4,128,128]{4,3,2,1,0:T(8,128)(2,1)} %get-tuple-element.171), calls=%async_computation.1 | async-start | bytes 8388608 | tf_op jit(solution)/shard_map/cond/branch_1_fun/all_to_all | solution.py:458
  17.6 120.1 %copy-start.1 = (bf16[3,128,2560]{2,1,0:T(8,128)(2,1)S(1)}, bf16[3,128,2560]{2,1,0:T(8,128)(2,1)}, u32[]{:S(2)}) copy-start(bf16[3,128,2560]{2,1,0:T(8,128)(2,1)} %get-tuple-element.350.q_ref) | copy-start | bytes 5898244 | tf_op jit(solution)/shard_map/cond
  17.6 120.2 %copy-start.16 = (s32[20]{0:T(128)S(1)}, s32[20]{0:T(128)}, u32[]{:S(2)}) copy-start(s32[20]{0:T(128)} %get-tuple-element.344.reach) | copy-start | bytes 244 | tf_op jit(solution)/shard_map/cond
  17.7 50.5 %collective-permute-start.9 = (bf16[10,3,128,128]{3,2,1,0:T(8,128)(2,1)}, bf16[10,3,128,128]{3,2,1,0:T(8,128)(2,1)}, u32[]{:S(2)}, u32[]{:S(2)}) collective-permute-start(bf16[10,3,128,128]{3,2,1,0:T(8,128)(2,1)} %get-tuple-element.164), channel_id=1, source_target_pairs={{0,2},{1,3},{2,0},{3,1},{4,6},{5,7},{6,4},{7,5},{8,10},{9,11},{10,... | collective-permute-start | bytes 2949128 | tf_op jit(solution)/shard_map/cond/branch_1_fun/ppermute | solution.py:387
  18.0 108.0 %collective-permute-start.15 = (bf16[10,3,128,128]{3,2,1,0:T(8,128)(2,1)}, bf16[10,3,128,128]{3,2,1,0:T(8,128)(2,1)}, u32[]{:S(2)}, u32[]{:S(2)}) collective-permute-start(bf16[10,3,128,128]{3,2,1,0:T(8,128)(2,1)} %get-tuple-element.165), channel_id=1, source_target_pairs={{0,2},{1,3},{2,0},{3,1},{4,6},{5,7},{6,4},{7,5},{8,10},{9,11},{10,... | collective-permute-start | bytes 2949128 | tf_op jit(solution)/shard_map/cond/branch_1_fun/ppermute | solution.py:387
  19.2 111.8 %collective-permute-start.11 = (bf16[10,3,128,128]{3,2,1,0:T(8,128)(2,1)}, bf16[10,3,128,128]{3,2,1,0:T(8,128)(2,1)S(1)}, u32[]{:S(2)}, u32[]{:S(2)}) collective-permute-start(bf16[10,3,128,128]{3,2,1,0:T(8,128)(2,1)} %get-tuple-element.165), channel_id=1, source_target_pairs={{2,4},{3,5},{4,2},{5,3},{6,8},{7,9},{8,6},{9,7},{10,12},{11,13},{1... | collective-permute-start | bytes 2949128 | tf_op jit(solution)/shard_map/cond/branch_1_fun/ppermute | solution.py:387
  22.3 115.5 %collective-permute-start.14 = (bf16[2,128,2560]{2,1,0:T(8,128)(2,1)}, bf16[2,128,2560]{2,1,0:T(8,128)(2,1)}, u32[]{:S(2)}, u32[]{:S(2)}) collective-permute-start(bf16[2,128,2560]{2,1,0:T(8,128)(2,1)} %get-tuple-element.167), channel_id=1, source_target_pairs={{0,1},{1,0},{2,3},{3,2},{4,5},{5,4},{6,7},{7,6},{8,9},{9,8},{10,11... | collective-permute-start | bytes 3932168 | tf_op jit(solution)/shard_map/cond/branch_1_fun/ppermute | solution.py:387
  68.1 66.9 %collective-permute-start.10 = (bf16[10,3,128,128]{3,2,1,0:T(8,128)(2,1)}, bf16[10,3,128,128]{3,2,1,0:T(8,128)(2,1)}, u32[]{:S(2)}, u32[]{:S(2)}) collective-permute-start(bf16[10,3,128,128]{3,2,1,0:T(8,128)(2,1)} %collective-permute-done.9.hk_ref), channel_id=1, source_target_pairs={{0,4},{1,5},{4,8},{5,9},{6,2},{7,3},{8,12},{9,13},{10,6},{11,7},{1... | collective-permute-start | bytes 2949128 | tf_op jit(solution)/shard_map/cond/branch_1_fun/ppermute | solution.py:387
  95.8 42.0 %collective-permute-start.16 = (bf16[10,128,128]{2,1,0:T(8,128)(2,1)}, bf16[10,128,128]{2,1,0:T(8,128)(2,1)}, u32[]{:S(2)}, u32[]{:S(2)}) collective-permute-start(bf16[10,128,128]{2,1,0:T(8,128)(2,1)} %dynamic-slice_bitcast_fusion.5), channel_id=1, source_target_pairs={{0,1},{1,0},{2,3},{3,2},{4,5},{5,4},{6,7},{7,6},{8,9},{9,8},{10,11... | collective-permute-start | bytes 983048 | tf_op jit(solution)/shard_map/cond/branch_1_fun/ppermute | solution.py:387
  127.8 10.0 %collective-permute-start.17 = (bf16[10,128,128]{2,1,0:T(8,128)(2,1)}, bf16[10,128,128]{2,1,0:T(8,128)(2,1)}, u32[]{:S(2)}, u32[]{:S(2)}) collective-permute-start(bf16[10,128,128]{2,1,0:T(8,128)(2,1)} %dynamic-slice_bitcast_fusion.4), channel_id=1, source_target_pairs={{0,1},{1,0},{2,3},{3,2},{4,5},{5,4},{6,7},{7,6},{8,9},{9,8},{10,11... | collective-permute-start | bytes 983048 | tf_op jit(solution)/shard_map/cond/branch_1_fun/ppermute | solution.py:387
  131.0 29.0 %copy-start.8 = (bf16[10,3,128,128]{3,2,1,0:T(8,128)(2,1)}, bf16[10,3,128,128]{3,2,1,0:T(8,128)(2,1)S(1)}, u32[]{:S(2)}) copy-start(bf16[10,3,128,128]{3,2,1,0:T(8,128)(2,1)S(1)} %collective-permute-done.11.hv_ref) | copy-start | bytes 2949124 | tf_op jit(solution)/shard_map/cond
  131.8 40.2 %collective-permute-start.13 = (bf16[10,128,128]{2,1,0:T(8,128)(2,1)}, bf16[10,128,128]{2,1,0:T(8,128)(2,1)S(1)}, u32[]{:S(2)}, u32[]{:S(2)}) collective-permute-start(bf16[10,128,128]{2,1,0:T(8,128)(2,1)} %dynamic-slice_bitcast_fusion.6), channel_id=1, source_target_pairs={{0,1},{1,0},{2,3},{3,2},{4,5},{5,4},{6,7},{7,6},{8,9},{9,8},{10,11... | collective-permute-start | bytes 983048 | tf_op jit(solution)/shard_map/cond/branch_1_fun/ppermute | solution.py:387
  136.8 35.2 %collective-permute-start.12 = (bf16[10,128,128]{2,1,0:T(8,128)(2,1)}, bf16[10,128,128]{2,1,0:T(8,128)(2,1)}, u32[]{:S(2)}, u32[]{:S(2)}) collective-permute-start(bf16[10,128,128]{2,1,0:T(8,128)(2,1)} %dynamic-slice_bitcast_fusion.7), channel_id=1, source_target_pairs={{0,1},{1,0},{2,3},{3,2},{4,5},{5,4},{6,7},{7,6},{8,9},{9,8},{10,11... | collective-permute-start | bytes 983048 | tf_op jit(solution)/shard_map/cond/branch_1_fun/ppermute | solution.py:387
  172.0 0.7 copy-start.14
